TPU v7x, 32 devices: a whole 2x2x4 slice. The times are simulated.
32 devices in a mesh: dp: 4 (over y, x), ctx: 8 (over z, core).
Axes of the slice: x: 2, y: 2, z: 4, core: 2. Of those that a mesh axis runs over, the one named last changes fastest.
Arguments:
- inputs: float32 [4, 1024, 1088], P('dp', 'ctx'), may hold values from -6 to 6
- out_grad: float32 [4, 1024, 1088], P('dp', 'ctx'), may hold values from -6 to 6
- pair_blocks: int32 [8, 2], replicated, may hold values from 0 to 15, as said below
- triple_weight: float32 [1088, 3264], P('ctx', 'dp')
- merge_weight: float32 [1088, 1088], P('ctx', 'dp'), may hold values from -0.75 to 0.75
- expand_weight: float32 [1088, 4352], P('ctx', 'dp'), may hold values from -0.1875 to 0.1875
- shrink_weight: float32 [4352, 1088], P('ctx', 'dp'), may hold values from -0.09375 to 0.09375
- vector_params: float32 [1088, 12], P('ctx', 'dp')
- triple_moment: float32 [1088, 3264], P('ctx', 'dp'), may hold values from -24 to 24
- merge_moment: float32 [1088, 1088], P('ctx', 'dp'), may hold values from -6 to 6
- expand_moment: float32 [1088, 4352], P('ctx', 'dp'), may hold values from -6 to 6
- shrink_moment: float32 [4352, 1088], P('ctx', 'dp'), may hold values from -6 to 6
- vector_moment: float32 [1088, 12], P('ctx', 'dp'), may hold values from -112 to 112
- triple_square: float32 [1088, 3264], P('ctx', 'dp'), may hold values from 24.576 to 245.76
- merge_square: float32 [1088, 1088], P('ctx', 'dp'), may hold values from 8.192 to 81.92
- expand_square: float32 [1088, 4352], P('ctx', 'dp'), may hold values from 8.192 to 81.92
- shrink_square: float32 [4352, 1088], P('ctx', 'dp'), may hold values from 8.192 to 81.92
- vector_square: float32 [1088, 12], P('ctx', 'dp'), may hold values from 204.8 to 2048
Outputs:
- block_output: float32 [4, 1024, 1088], P('dp', 'ctx')
- input_grad: float32 [4, 1024, 1088], P('dp', 'ctx')
- triple_grad: float32 [1088, 3264], P('ctx', 'dp')
- merge_grad: float32 [1088, 1088], P('ctx', 'dp')
- expand_grad: float32 [1088, 4352], P('ctx', 'dp')
- shrink_grad: float32 [4352, 1088], P('ctx', 'dp')
- vector_grad: float32 [1088, 12], P('ctx', 'dp')
- triple_new: float32 [1088, 3264], P('ctx', 'dp')
- merge_new: float32 [1088, 1088], P('ctx', 'dp')
- expand_new: float32 [1088, 4352], P('ctx', 'dp')
- shrink_new: float32 [4352, 1088], P('ctx', 'dp')
- vector_new: float32 [1088, 12], P('ctx', 'dp')
- triple_moment_new: float32 [1088, 3264], P('ctx', 'dp')
- merge_moment_new: float32 [1088, 1088], P('ctx', 'dp')
- expand_moment_new: float32 [1088, 4352], P('ctx', 'dp')
- shrink_moment_new: float32 [4352, 1088], P('ctx', 'dp')
- vector_moment_new: float32 [1088, 12], P('ctx', 'dp')
- triple_square_new: float32 [1088, 3264], P('ctx', 'dp')
- merge_square_new: float32 [1088, 1088], P('ctx', 'dp')
- expand_square_new: float32 [1088, 4352], P('ctx', 'dp')
- shrink_square_new: float32 [4352, 1088], P('ctx', 'dp')
- vector_square_new: float32 [1088, 12], P('ctx', 'dp')
Inputs may be any that keep to these rules, and one draw needn't show every extreme that they name: `pair_blocks`: row c names the two blocks of 64 positions that stand in stored rows c * 2 * 64 onward: first a block p, then 2 * 8 - 1 - p; each of the 16 blocks is named once.
All inputs are finite; a program needn't handle non-finite values.
Results may differ from a plain program's by a relative error of at most 0.011.
Values may be sent and summed in bfloat16 or wider, within the bound.
A program may use at most 256 MiB of HBM per device.

v0:
```python
import jax
import jax.numpy as jnp
from jax import lax
from jax.experimental import pallas as pl
from jax.experimental.pallas import tpu as pltpu
from jax.sharding import PartitionSpec as P

D = 1088
H = 17
HD = 64
BLK = 64


norm_eps = 1e-05
beta_first = 0.9
beta_second = 0.95
learn_rate = 0.01
decay_rate = 0.1
adam_eps = 1e-08
adam_steps = 4
gelu_coef = 0.7978845608028654
masked_score = -1e30


def layer_norm(values):
    center = jnp.mean(values, axis=-1, keepdims=True)
    shifted = values - center
    inverse = lax.rsqrt(jnp.mean(shifted * shifted, axis=-1, keepdims=True) + norm_eps)
    return (shifted * inverse, inverse)


def norm_back(incoming, normed, inverse, gain_vec):
    scaled = incoming * gain_vec
    return inverse * (
        scaled
        - jnp.mean(scaled, axis=-1, keepdims=True)
        - normed * jnp.mean(scaled * normed, axis=-1, keepdims=True)
    )


def gelu_value(values):
    inside = gelu_coef * (values + 0.044715 * values * values * values)
    return 0.5 * values * (1.0 + jnp.tanh(inside))


def gelu_slope(values):
    inside = gelu_coef * (values + 0.044715 * values * values * values)
    tangent = jnp.tanh(inside)
    return 0.5 * (1.0 + tangent) + 0.5 * values * (1.0 - tangent * tangent) * gelu_coef * (
        1.0 + 3.0 * 0.044715 * values * values
    )


def adam_update(weight, gradient, moment, square, decayed):
    moment_new = beta_first * moment + (1.0 - beta_first) * gradient
    square_new = beta_second * square + (1.0 - beta_second) * gradient * gradient
    first_fix = 1.0 - beta_first**adam_steps
    second_fix = 1.0 - beta_second**adam_steps
    direction = moment_new / first_fix / (jnp.sqrt(square_new / second_fix) + adam_eps)
    if decayed:
        direction = direction + decay_rate * weight
    return (weight - learn_rate * direction, moment_new, square_new)


def dot_on(left, right, left_dim, right_dim):
    return lax.dot_general(
        left, right, (((left_dim,), (right_dim,)), ((), ())), preferred_element_type=jnp.float32
    )


def head_probs(query_t, key_t, allowed):
    scores = dot_on(query_t, key_t, 0, 0) * HD ** (-0.5)
    scores = jnp.where(allowed, scores, masked_score)
    row_max = jnp.max(scores, axis=1, keepdims=True)
    weights = jnp.exp(scores - row_max)
    return weights / jnp.sum(weights, axis=1, keepdims=True)


def forward_kernel(query_pos, key_pos, query_ref, key_ref, value_ref, out_ref):
    allowed = query_pos[...] >= key_pos[...]
    probs = head_probs(query_ref[...], key_ref[...], allowed).astype(jnp.bfloat16)
    out_ref[...] = dot_on(value_ref[...], probs, 1, 1).astype(jnp.bfloat16)


def backward_kernel(
    query_pos, key_pos, query_ref, key_ref, value_ref, out_ref, dout_ref, dquery, dkey, dvalue
):
    allowed = query_pos[...] >= key_pos[...]
    query_t = query_ref[...]
    key_t = key_ref[...]
    dout_t = dout_ref[...]
    probs = head_probs(query_t, key_t, allowed)
    dprobs = dot_on(dout_t, value_ref[...], 0, 0)
    products = dout_t.astype(jnp.float32) * out_ref[...].astype(jnp.float32)
    delta = jnp.sum(products.T, axis=1, keepdims=True)
    dscores = (probs * (dprobs - delta) * HD ** (-0.5)).astype(jnp.bfloat16)
    dquery[...] = dot_on(key_t, dscores, 1, 1).astype(jnp.bfloat16)
    dkey[...] = dot_on(query_t, dscores, 1, 0).astype(jnp.bfloat16)
    dvalue[...] = dot_on(dout_t, probs.astype(jnp.bfloat16), 1, 0).astype(jnp.bfloat16)


def attention(kernel, query_pos, key_pos, features, out_rows):
    queries, keys = query_pos.shape[0], key_pos.shape[1]
    whole = lambda array: pl.BlockSpec(array.shape, lambda h: (0, 0))
    block = lambda width: pl.BlockSpec((HD, width), lambda h: (h, 0))
    shapes = [jax.ShapeDtypeStruct((H * HD, width), jnp.bfloat16) for width in out_rows]
    flops = 2 * H * HD * queries * keys * (2 if len(out_rows) == 1 else 5)
    return pl.pallas_call(
        kernel,
        grid=(H,),
        in_specs=[whole(query_pos), whole(key_pos)] + [block(x.shape[1]) for x in features],
        out_specs=[block(width) for width in out_rows],
        out_shape=shapes,
        cost_estimate=pl.CostEstimate(
            flops=flops, bytes_accessed=8 * H * HD * keys, transcendentals=H * queries * keys
        ),
    )(query_pos, key_pos, *features)


def exchange(blocks):
    return lax.all_to_all(blocks, "ctx", split_axis=0, concat_axis=0, tiled=True)


def scatter_rows(partial):
    return lax.psum_scatter(
        partial.astype(jnp.bfloat16), "ctx", scatter_dimension=0, tiled=True
    ).astype(jnp.float32)


def gather_rows(rows):
    return lax.all_gather(rows, "ctx", axis=0, tiled=True)


def local(
    inputs,
    out_grad,
    pair_blocks,
    triple_weight,
    merge_weight,
    expand_weight,
    shrink_weight,
    vector_params,
    triple_moment,
    merge_moment,
    expand_moment,
    shrink_moment,
    vector_moment,
    triple_square,
    merge_square,
    expand_square,
    shrink_square,
    vector_square,
):
    bf16 = jnp.bfloat16
    n = lax.axis_size("ctx")
    m = lax.axis_size("dp")
    here = lax.axis_index("ctx")
    rows = inputs.shape[1]
    total = rows * n
    feat = D // n
    hidden_width = m * expand_weight.shape[1]
    wide = hidden_width // n
    stream = inputs[0]
    cotangent = out_grad[0]
    offsets = jnp.arange(BLK, dtype=jnp.int32)
    positions = (pair_blocks.reshape(-1)[:, None] * BLK + offsets[None, :]).reshape(-1)
    query_pos = lax.dynamic_slice_in_dim(positions, here * rows, rows)[:, None]
    key_pos = positions[None, :]

    packed = jnp.concatenate(
        [
            triple_weight.astype(bf16),
            merge_weight.astype(bf16),
            expand_weight.astype(bf16),
            vector_params.astype(bf16),
        ],
        axis=1,
    )
    tw, mw, ew = triple_weight.shape[1], merge_weight.shape[1], expand_weight.shape[1]
    columns = lax.all_gather(packed, "dp", axis=0)

    def take(start, width):
        return columns[:, :, start : start + width].transpose(1, 0, 2).reshape(feat, m * width)

    triple_rows = take(0, tw)
    merge_rows = take(tw, mw)
    expand_rows = take(tw + mw, ew)
    vector_rows = take(tw + mw + ew, vector_params.shape[1])
    normed_one, inverse_one = layer_norm(stream)
    normed_full = gather_rows(normed_one.astype(bf16))
    send = jnp.concatenate(
        [
            triple_rows.reshape(feat, 3, n, feat).transpose(2, 0, 1, 3).reshape(n, feat, 3 * feat),
            expand_rows.reshape(feat, n, wide).transpose(1, 0, 2),
        ],
        axis=2,
    )
    got = exchange(send).reshape(D, 3 * feat + wide)
    w_triple = got[:, : 3 * feat]
    w_expand = got[:, 3 * feat :]
    merged = gather_rows(jnp.concatenate([merge_rows, vector_rows], axis=1))
    w_merge = merged[:, :D]
    vectors = merged[:, D:].astype(jnp.float32)
    gain_one = vectors[:, 0]
    shift_one = vectors[:, 1]
    query_bias = lax.dynamic_slice_in_dim(vectors[:, 2], here * feat, feat)
    value_bias = lax.dynamic_slice_in_dim(vectors[:, 3], here * feat, feat)
    merge_bias = vectors[:, 4]
    gain_two = vectors[:, 5]
    shift_two = vectors[:, 6]
    shrink_bias = vectors[:, 7]
    expand_bias = lax.dynamic_slice_in_dim(vectors[:, 8:].T.reshape(-1), here * wide, wide)

    act_one = (normed_full.astype(jnp.float32) * gain_one + shift_one).astype(bf16)
    bias = jnp.concatenate([query_bias, jnp.zeros_like(query_bias), value_bias])
    triple_t = (dot_on(w_triple, act_one, 0, 1) + bias[:, None]).astype(bf16)
    query_t = exchange(triple_t[:feat].reshape(feat, n, rows).transpose(1, 0, 2)).reshape(D, rows)
    both = lax.all_gather(triple_t[feat:].reshape(2, feat, total), "ctx", axis=0)
    key_t = both[:, 0].reshape(D, total)
    value_t = both[:, 1].reshape(D, total)
    (attended_t,) = attention(
        forward_kernel, query_pos, key_pos, (query_t, key_t, value_t), (rows,)
    )
    cot_full = gather_rows(cotangent.astype(bf16))
    w_shrink = (
        lax.all_gather(shrink_weight.astype(bf16), "dp", axis=0).transpose(1, 0, 2).reshape(wide, D)
    )
    middle = stream + dot_on(attended_t, w_merge, 0, 0) + merge_bias
    normed_two, inverse_two = layer_norm(middle)
    act_two = gather_rows((normed_two * gain_two + shift_two).astype(bf16))
    pre_act = dot_on(act_two, w_expand, 1, 0) + expand_bias
    hidden_b = gelu_value(pre_act).astype(bf16)
    dpre = dot_on(cot_full, w_shrink, 1, 1) * gelu_slope(pre_act)
    dpre_b = dpre.astype(bf16)
    expand_bias_grad = jnp.sum(dpre, axis=0)
    dact_two = scatter_rows(dot_on(dpre_b, w_expand, 1, 1))
    block_out = middle + scatter_rows(dot_on(hidden_b, w_shrink, 1, 0)) + shrink_bias
    shrink_part = dot_on(hidden_b, cot_full, 0, 0).astype(bf16)
    expand_part = dot_on(act_two, dpre_b, 0, 0).astype(bf16)
    shrink_grad = lax.psum_scatter(
        shrink_part.reshape(wide, m, D // m).transpose(1, 0, 2), "dp", scatter_dimension=0
    ).astype(jnp.float32)
    shrink_bias_grad = jnp.sum(cotangent, axis=0)
    gain_two_grad = jnp.sum(dact_two * normed_two, axis=0)
    shift_two_grad = jnp.sum(dact_two, axis=0)
    dmiddle = cotangent + norm_back(dact_two, normed_two, inverse_two, gain_two)
    dmiddle_b = dmiddle.astype(bf16)
    merge_part = lax.psum_scatter(
        dot_on(attended_t, dmiddle_b, 1, 0).astype(bf16), "ctx", scatter_dimension=0, tiled=True
    )
    merge_bias_grad = jnp.sum(dmiddle, axis=0)
    dattended_t = dot_on(w_merge, dmiddle_b, 1, 1).astype(bf16)
    dquery_t, dkey_t, dvalue_t = attention(
        backward_kernel,
        query_pos,
        key_pos,
        (query_t, key_t, value_t, attended_t, dattended_t),
        (rows, total, total),
    )
    dquery_c = exchange(dquery_t.reshape(n, feat, rows)).transpose(1, 0, 2).reshape(feat, total)
    dkey_c = lax.psum_scatter(dkey_t, "ctx", scatter_dimension=0, tiled=True)
    dvalue_c = lax.psum_scatter(dvalue_t, "ctx", scatter_dimension=0, tiled=True)
    dtriple_t = jnp.concatenate([dquery_c, dkey_c, dvalue_c], axis=0)
    query_bias_grad = jnp.sum(dquery_c.astype(jnp.float32), axis=1)
    value_bias_grad = jnp.sum(dvalue_c.astype(jnp.float32), axis=1)
    dact_one = scatter_rows(dot_on(dtriple_t, w_triple, 0, 1))
    triple_part = dot_on(act_one, dtriple_t, 0, 1).astype(bf16)
    gain_one_grad = jnp.sum(dact_one * normed_one, axis=0)
    shift_one_grad = jnp.sum(dact_one, axis=0)
    input_rows = dmiddle + norm_back(dact_one, normed_one, inverse_one, gain_one)

    def place(piece, size):
        return lax.dynamic_update_slice_in_dim(
            jnp.zeros((size,), jnp.float32), piece, here * piece.shape[0], 0
        )

    vector_local = jnp.concatenate(
        [
            jnp.stack(
                [
                    gain_one_grad,
                    shift_one_grad,
                    place(query_bias_grad, D),
                    place(value_bias_grad, D),
                    merge_bias_grad,
                    gain_two_grad,
                    shift_two_grad,
                    shrink_bias_grad,
                ],
                axis=1,
            ),
            place(expand_bias_grad, hidden_width).reshape(-1, D).T,
        ],
        axis=1,
    )
    vector_part = lax.psum_scatter(vector_local, "ctx", scatter_dimension=0, tiled=True)

    def by_dp(rows_part):
        return rows_part.reshape(feat, m, -1).transpose(1, 0, 2)

    expand_rows_part = exchange(expand_part.reshape(n, feat, wide)).transpose(1, 0, 2)
    expand_grad = lax.psum_scatter(by_dp(expand_rows_part), "dp", scatter_dimension=0).astype(
        jnp.float32
    )
    triple_rows_part = (
        exchange(triple_part.reshape(n, feat, 3 * feat))
        .reshape(n, feat, 3, feat)
        .transpose(1, 2, 0, 3)
    )
    last = lax.psum_scatter(
        jnp.concatenate(
            [by_dp(triple_rows_part), by_dp(merge_part), by_dp(vector_part).astype(bf16)], axis=2
        ),
        "dp",
        scatter_dimension=0,
    ).astype(jnp.float32)
    triple_grad = last[:, :tw]
    merge_grad = last[:, tw : tw + mw]
    vector_grad = last[:, tw + mw :]
    triple_new, triple_moment_new, triple_square_new = adam_update(
        triple_weight, triple_grad, triple_moment, triple_square, True
    )
    merge_new, merge_moment_new, merge_square_new = adam_update(
        merge_weight, merge_grad, merge_moment, merge_square, True
    )
    expand_new, expand_moment_new, expand_square_new = adam_update(
        expand_weight, expand_grad, expand_moment, expand_square, True
    )
    shrink_new, shrink_moment_new, shrink_square_new = adam_update(
        shrink_weight, shrink_grad, shrink_moment, shrink_square, True
    )
    vector_new, vector_moment_new, vector_square_new = adam_update(
        vector_params, vector_grad, vector_moment, vector_square, False
    )
    return (
        block_out[None],
        input_rows[None],
        triple_grad,
        merge_grad,
        expand_grad,
        shrink_grad,
        vector_grad,
        triple_new,
        merge_new,
        expand_new,
        shrink_new,
        vector_new,
        triple_moment_new,
        merge_moment_new,
        expand_moment_new,
        shrink_moment_new,
        vector_moment_new,
        triple_square_new,
        merge_square_new,
        expand_square_new,
        shrink_square_new,
        vector_square_new,
    )


def solution(mesh):
    in_specs = (
        P("dp", "ctx", None),
        P("dp", "ctx", None),
        P(),
        P("ctx", "dp"),
        P("ctx", "dp"),
        P("ctx", "dp"),
        P("ctx", "dp"),
        P("ctx", "dp"),
        P("ctx", "dp"),
        P("ctx", "dp"),
        P("ctx", "dp"),
        P("ctx", "dp"),
        P("ctx", "dp"),
        P("ctx", "dp"),
        P("ctx", "dp"),
        P("ctx", "dp"),
        P("ctx", "dp"),
        P("ctx", "dp"),
    )
    out_specs = (
        P("dp", "ctx", None),
        P("dp", "ctx", None),
        P("ctx", "dp"),
        P("ctx", "dp"),
        P("ctx", "dp"),
        P("ctx", "dp"),
        P("ctx", "dp"),
        P("ctx", "dp"),
        P("ctx", "dp"),
        P("ctx", "dp"),
        P("ctx", "dp"),
        P("ctx", "dp"),
        P("ctx", "dp"),
        P("ctx", "dp"),
        P("ctx", "dp"),
        P("ctx", "dp"),
        P("ctx", "dp"),
        P("ctx", "dp"),
        P("ctx", "dp"),
        P("ctx", "dp"),
        P("ctx", "dp"),
        P("ctx", "dp"),
    )
    return jax.shard_map(local, mesh=mesh, in_specs=in_specs, out_specs=out_specs, check_vma=False)
```

profile of v0, /device:TPU:9, one launch (start us, length us, event | category | flops | bytes accessed | tf_op | source)
XLA Modules:
  0.0 781.1 jit_solution(6894993608539550052)
XLA Ops:
  12.9 39.7 %all-gather.21.cloned.1.call-done = bf16[544,2179]{1,0:T(8,128)(2,1)} async-done(((bf16[136,2179]{1,0:T(8,128)(2,1)}), bf16[544,2179]{1,0:T(8,128)(2,1)}) %all-gather.21.cloned.1.call-update) | async-done | bytes 2370768 | tf_op jit(solution)/shard_map/all_gather | solution.py:180
  61.5 1.7 reshape_reshape.7
  64.8 2.4 reshape_reshape.6
  67.2 2.6 copy.188
  69.9 3.0 copy.190
  73.8 2.7 copy.191
  76.4 5.6 all-to-all-start
  82.0 14.4 %all-gather.13.cloned.1.call-done = bf16[1088,1100]{1,0:T(8,128)(2,1)} async-done(((bf16[136,1100]{1,0:T(8,128)(2,1)}), bf16[1088,1100]{1,0:T(8,128)(2,1)}) %all-gather.13.cloned.1.call-update) | async-done | bytes 2393616 | tf_op jit(solution)/shard_map/all_gather | solution.py:131
  97.5 2.0 slice_reduce_fusion
  99.8 54.4 %all-gather.11.cloned.1.call-done = bf16[1024,1088]{0,1:T(8,128)(2,1)} async-done(((bf16[128,1088]{0,1:T(8,128)(2,1)}), bf16[1024,1088]{0,1:T(8,128)(2,1)}) %all-gather.11.cloned.1.call-update) | async-done | bytes 2228240 | tf_op jit(solution)/shard_map/all_gather | solution.py:131
  154.2 3.9 add_convert_fusion.1
  160.3 1.7 bitcast_bitcast_fusion
  162.0 5.5 all-to-all-start.1
  168.6 43.6 %all-gather.15.cloned.1.call-done = bf16[8,2,136,1024]{3,2,0,1:T(8,128)(2,1)} async-done(((bf16[1,2,136,1024]{3,2,0,1:T(8,128)(2,1)}), bf16[8,2,136,1024]{3,2,0,1:T(8,128)(2,1)}) %all-gather.15.cloned.1.call-update) | async-done | bytes 4456464 | tf_op jit(solution)/shard_map/all_gather | solution.py:218
  212.2 4.9 fusion.49
  217.8 16.2 %shard_map.345.out_ref = bf16[1088,128]{1,0:T(8,128)(2,1)} custom-call(s32[128,1]{1,0:T(8,128)} %copy.197.query_pos, s32[1,1024]{1,0:T(1,128)} %add.235.key_pos, bf16[1088,128]{1,0:T(8,128)(2,1)} %bitcast.139, bf16[1088,1024]{1,0:T(8,128)(2,1)} %bitcast.122, bf16[1088,1024]{1,0:T(8,128)(2,1)} %bitcast.120), custom_call_target="tpu_custom_call" | custom-call | flops 570425344 | bytes 8912896 | tf_op jit(solution)/shard_map/pallas_call | solution.py:108
  234.0 3.0 fusion.51
  239.8 33.6 %all-gather.17.cloned.1.call-done = bf16[1024,1088]{0,1:T(8,128)(2,1)} async-done(((bf16[128,1088]{0,1:T(8,128)(2,1)}), bf16[1024,1088]{0,1:T(8,128)(2,1)}) %all-gather.17.cloned.1.call-update) | async-done | bytes 2228240 | tf_op jit(solution)/shard_map/all_gather | solution.py:131
  273.4 5.8 fusion.10
  279.2 26.9 %all-gather.19.cloned.1.call-done = bf16[1024,1088]{0,1:T(8,128)(2,1)} async-done(((bf16[128,1088]{0,1:T(8,128)(2,1)}), bf16[1024,1088]{0,1:T(8,128)(2,1)}) %all-gather.19.cloned.1.call-update) | async-done | bytes 2228240 | tf_op jit(solution)/shard_map/all_gather | solution.py:131
  306.0 5.5 convolution_convert_fusion.4
  311.5 2.6 copy.210
  314.2 27.7 %reduce-scatter.41.cloned.1.call-done = bf16[1,544,272]{1,2,0:T(8,128)(2,1)} async-done(((bf16[4,544,272]{1,2,0:T(8,128)(2,1)}), bf16[1,544,272]{1,2,0:T(8,128)(2,1)}) %reduce-scatter.41.cloned.1.call-update) | async-done | bytes 295952
  341.9 3.2 multiply_subtract_fusion.1
  345.6 29.1 %all-gather.23.cloned.1.call-done = bf16[4,544,272]{1,2,0:T(8,128)(2,1)} async-done(((bf16[1,544,272]{1,2,0:T(8,128)(2,1)}), bf16[4,544,272]{1,2,0:T(8,128)(2,1)}) %all-gather.23.cloned.1.call-update) | async-done | bytes 1183760 | tf_op jit(solution)/shard_map/all_gather | solution.py:226
  374.6 5.8 fusion.52
  381.5 3.3 convolution_convert_fusion.1
  384.8 4.2 copy.229
  389.1 5.6 convolution_convert_fusion.2
  394.7 4.2 copy.227
  398.9 22.7 %reduce-scatter.31.cloned.1.call-done = bf16[128,1088]{1,0:T(8,128)(2,1)} async-done(((bf16[1024,1088]{1,0:T(8,128)(2,1)}), bf16[128,1088]{1,0:T(8,128)(2,1)}) %reduce-scatter.31.cloned.1.call-update) | async-done | bytes 278544
  423.3 36.6 %reduce-scatter.29.cloned.1.call-done = bf16[128,1088]{1,0:T(8,128)(2,1)} async-done(((bf16[1024,1088]{1,0:T(8,128)(2,1)}), bf16[128,1088]{1,0:T(8,128)(2,1)}) %reduce-scatter.29.cloned.1.call-update) | async-done | bytes 278544
  464.5 18.3 %shard_map.346 = (bf16[1088,128]{1,0:T(8,128)(2,1)}, bf16[1088,1024]{1,0:T(8,128)(2,1)}, bf16[1088,1024]{1,0:T(8,128)(2,1)}) custom-call(s32[128,1]{1,0:T(8,128)} %copy.197.query_pos, s32[1,1024]{1,0:T(1,128)} %add.235.key_pos, bf16[1088,128]{1,0:T(8,128)(2,1)} %bitcast.140, bf16[1088,1024]{1,0:T(8,128)(2,1)} %bitcast.123, bf16[1088,1024]{1,0:T(8,128)(2,1)} %bitcast.121, ...), custom_call_target="tpu_custom_call" | custom-call | flops 1426063360 | bytes 8912896 | tf_op jit(solution)/shard_map/pallas_call | solution.py:108
  483.7 2.3 convolution_convert_fusion
  486.0 21.2 %all_to_all.25 = bf16[8,136,128]{2,1,0:T(8,128)(2,1)S(1)} all-to-all(bf16[8,136,128]{2,1,0:T(8,128)(2,1)S(1)} %bitcast.149), channel_id=1, replica_groups=mesh['dp'=4,'ctx'=8] {'ctx'}, dimensions={0} | all-to-all | bytes 557056 | tf_op jit(solution)/shard_map/all_to_all | solution.py:121
  507.3 17.8 %reduce-scatter.25.cloned.1.call-done = bf16[136,1024]{1,0:T(8,128)(2,1)} async-done(((bf16[1088,1024]{1,0:T(8,128)(2,1)}), bf16[136,1024]{1,0:T(8,128)(2,1)}) %reduce-scatter.25.cloned.1.call-update) | async-done | bytes 278544 | tf_op jit(solution)/shard_map/reduce_scatter | solution.py:261
  526.1 32.4 %reduce-scatter.27.cloned.1.call-done = bf16[136,1024]{1,0:T(8,128)(2,1)} async-done(((bf16[1088,1024]{1,0:T(8,128)(2,1)}), bf16[136,1024]{1,0:T(8,128)(2,1)}) %reduce-scatter.27.cloned.1.call-update) | async-done | bytes 278544 | tf_op jit(solution)/shard_map/reduce_scatter | solution.py:262
  559.5 4.3 convolution_convert_fusion.3
  563.8 4.2 copy.231
  569.3 4.3 convolution_convert_fusion.5
  573.6 2.4 copy.207
  576.0 51.4 %all_to_all.26 = bf16[8,136,544]{2,1,0:T(8,128)(2,1)S(1)} all-to-all(bf16[8,136,544]{2,1,0:T(8,128)(2,1)S(1)} %bitcast.129), channel_id=1, replica_groups=mesh['dp'=4,'ctx'=8] {'ctx'}, dimensions={0} | all-to-all | bytes 2367488 | tf_op jit(solution)/shard_map/all_to_all | solution.py:121
  627.6 1.8 reshape.211
  629.4 2.5 copy.209
  631.9 3.2 convolution_convert_fusion.6
  636.8 5.5 all-to-all-start.3
  644.9 2.1 reshape.208
  647.0 32.5 %all-to-all-done.3 = bf16[8,136,408]{2,1,0:T(8,128)(2,1)S(1)} async-done(((bf16[8,136,408]{2,1,0:T(8,128)(2,1)}), bf16[8,136,408]{2,1,0:T(8,128)(2,1)S(1)}, u32[]{:S(2)}, u32[]{:S(2)}) %all-to-all-start.3) | async-done | bytes 887840 | tf_op jit(solution)/shard_map/all_to_all | solution.py:121
  681.2 3.1 copy.203
  684.3 2.9 reshape.207
  689.1 24.4 %all-reduce.1 = bf16[1088,12]{0,1:T(8,128)(2,1)S(1)} all-reduce(f32[1088,12]{0,1:T(8,128)S(1)} %concatenate.26), channel_id=10, replica_groups=mesh['dp'=4,'ctx'=8] {'ctx'}, use_global_device_ids=true, to_apply=%region_23.0.clone | all-reduce | flops 13056 | bytes 78336
  713.7 4.6 concatenate.27
  721.0 2.3 copy.212
  723.3 1.8 copy.215
  725.1 1.8 copy.216
  726.8 3.1 multiply_subtract_fusion.2
  731.0 22.3 %reduce-scatter.37.cloned.1.call-done = bf16[1,136,1091]{2,1,0:T(8,128)(2,1)} async-done(((bf16[4,136,1091]{2,1,0:T(8,128)(2,1)}), bf16[1,136,1091]{2,1,0:T(8,128)(2,1)}) %reduce-scatter.37.cloned.1.call-update) | async-done | bytes 296768
  753.4 2.0 copy.206
  756.5 3.2 multiply_subtract_fusion
  759.8 2.2 copy.219
  762.0 2.1 multiply_subtract_fusion.3
  764.0 1.9 copy.220
  765.9 2.2 copy.221
  768.2 1.8 copy.222
  (197 shorter events, 53.5 us)
Async XLA Ops:
  7.2 45.4 %all-gather.21.cloned.1.call-start = ((), (), s32[]{:S(2)}) async-start(), calls=%async_computation.21 | async-start | bytes 3133440 | tf_op jit(solution)/shard_map/all_gather | solution.py:180
  12.9 45.4 %copy-start = (f32[1,128,1088]{1,2,0:T(8,128)S(1)}, f32[1,128,1088]{1,2,0:T(8,128)}, u32[]{:S(2)}) copy-start(f32[1,128,1088]{1,2,0:T(8,128)} %param.18) | copy-start | bytes 1671172
  12.9 83.5 %all-gather.13.cloned.1.call-start = ((), (), s32[]{:S(2)}) async-start(), calls=%async_computation.15 | async-start | bytes 2820096 | tf_op jit(solution)/shard_map/all_gather | solution.py:131
  55.1 4.3 copy-start.5
  58.2 96.0 %all-gather.11.cloned.1.call-start = ((), (), s32[]{:S(2)}) async-start(), calls=%async_computation.14 | async-start | bytes 2506752 | tf_op jit(solution)/shard_map/all_gather | solution.py:131
  69.9 3.0 copy-start.1
  76.4 77.8 %all-to-all-start = ((bf16[8,136,952]{2,1,0:T(8,128)(2,1)}), bf16[8,136,952]{2,1,0:T(8,128)(2,1)S(1)}, u32[]{:S(2)}, u32[]{:S(2)}) async-start(bf16[8,136,952]{2,1,0:T(8,128)(2,1)} %copy.191), calls=%async_computation | async-start | bytes 4456448 | tf_op jit(solution)/shard_map/all_to_all | solution.py:121
  82.0 130.2 %all-gather.15.cloned.1.call-start = ((), (), s32[]{:S(2)}) async-start(), calls=%async_computation.16 | async-start | bytes 5013504 | tf_op jit(solution)/shard_map/all_gather | solution.py:218
  154.2 3.9 copy-start.10
  154.2 5.1 copy-start.29
  158.1 1.1 copy-start.19
  162.0 55.1 %all-to-all-start.1 = ((bf16[8,136,128]{2,1,0:T(8,128)(2,1)}), bf16[8,136,128]{2,1,0:T(8,128)(2,1)S(1)}, u32[]{:S(2)}, u32[]{:S(2)}) async-start(bf16[8,136,128]{2,1,0:T(8,128)(2,1)} %bitcast_bitcast_fusion), calls=%async_computation.1 | async-start | bytes 557056 | tf_op jit(solution)/shard_map/all_to_all | solution.py:121
  167.6 105.8 %all-gather.17.cloned.1.call-start = ((), (), s32[]{:S(2)}) async-start(), calls=%async_computation.17 | async-start | bytes 2506752 | tf_op jit(solution)/shard_map/all_gather | solution.py:131
  217.1 0.7 copy-start.7
  234.0 4.3 copy-start.12
  238.3 67.8 %all-gather.19.cloned.1.call-start = ((), (), s32[]{:S(2)}) async-start(), calls=%async_computation.18 | async-start | bytes 2506752 | tf_op jit(solution)/shard_map/all_gather | solution.py:131
  239.1 102.8 %reduce-scatter.41.cloned.1.call-start = ((), (), s32[]{:S(2)}) async-start(), calls=%async_computation.29 | async-start | bytes 1740800
  311.5 30.4 %copy-start.21 = (f32[544,272]{0,1:T(8,128)S(1)}, f32[544,272]{0,1:T(8,128)}, u32[]{:S(2)}) copy-start(f32[544,272]{0,1:T(8,128)} %param.24) | copy-start | bytes 1775620
  314.1 60.5 %all-gather.23.cloned.1.call-start = ((), (), s32[]{:S(2)}) async-start(), calls=%async_computation.22 | async-start | bytes 1740800 | tf_op jit(solution)/shard_map/all_gather | solution.py:226
  345.1 76.5 %reduce-scatter.31.cloned.1.call-start = ((), (), s32[]{:S(2)}) async-start(), calls=%async_computation.24 | async-start | bytes 2654208
  374.6 6.9 copy-start.11
  380.4 1.0 copy-start.31
  389.0 70.8 %reduce-scatter.29.cloned.1.call-start = ((), (), s32[]{:S(2)}) async-start(), calls=%async_computation.23 | async-start | bytes 2654208
  398.9 126.2 %reduce-scatter.25.cloned.1.call-start = ((), (), s32[]{:S(2)}) async-start(), calls=%async_computation.19 | async-start | bytes 2506752 | tf_op jit(solution)/shard_map/reduce_scatter | solution.py:261
  461.0 1.9 copy-start.25
  482.7 1.0 copy-start.6
  482.7 75.8 %reduce-scatter.27.cloned.1.call-start = ((), (), s32[]{:S(2)}) async-start(), calls=%async_computation.20 | async-start | bytes 2506752 | tf_op jit(solution)/shard_map/reduce_scatter | solution.py:262
  483.3 2.7 copy-start.23
  483.3 161.5 %reduce-scatter.35.cloned.1.call-start = ((), (), s32[]{:S(2)}) async-start(), calls=%async_computation.26 | async-start | bytes 2820096
  486.0 201.2 %reduce-scatter.33.cloned.1.call-start = ((), (), s32[]{:S(2)}) async-start(), calls=%async_computation.25 | async-start | bytes 2654208
  559.5 4.3 copy-start.24
  568.0 1.2 copy-start.32
  568.0 158.8 %reduce-scatter.39.cloned.1.call-start = ((), (), s32[]{:S(2)}) async-start(), calls=%async_computation.28 | async-start | bytes 1566720
  635.2 7.1 copy-start.30
  635.2 9.2 %copy-start.18 = (bf16[136,1024]{1,0:T(8,128)(2,1)S(1)}, bf16[136,1024]{1,0:T(8,128)(2,1)}, u32[]{:S(2)}) copy-start(bf16[136,1024]{1,0:T(8,128)(2,1)} %reduce-scatter.27.cloned.1.call-done) | copy-start | bytes 835588
  636.8 42.7 %all-to-all-start.3 = ((bf16[8,136,408]{2,1,0:T(8,128)(2,1)}), bf16[8,136,408]{2,1,0:T(8,128)(2,1)S(1)}, u32[]{:S(2)}, u32[]{:S(2)}) async-start(bf16[8,136,408]{2,1,0:T(8,128)(2,1)} %bitcast.27), calls=%async_computation.5 | async-start | bytes 2228224 | tf_op jit(solution)/shard_map/all_to_all | solution.py:121
  642.3 111.1 %reduce-scatter.37.cloned.1.call-start = ((), (), s32[]{:S(2)}) async-start(), calls=%async_computation.27 | async-start | bytes 1566720
  687.2 26.5 %copy-start.2 = (bf16[136,4,816]{2,1,0:T(4,128)(2,1)S(1)}, bf16[136,4,816]{2,1,0:T(4,128)(2,1)}, u32[]{:S(2)}) copy-start(bf16[136,4,816]{2,1,0:T(4,128)(2,1)} %reshape.207) | copy-start | bytes 2663428
  688.5 25.3 %copy-start.8 = (bf16[128,1088]{0,1:T(8,128)(2,1)}, bf16[128,1088]{0,1:T(8,128)(2,1)S(1)}, u32[]{:S(2)}) copy-start(bf16[128,1088]{0,1:T(8,128)(2,1)S(1)} %copy.232) | copy-start | bytes 835588
  718.4 1.2 copy-start.13
  718.4 1.5 copy-start.20
  719.6 1.2 copy-start.22
  726.8 3.2 copy-start.9
  756.5 5.5 copy-start.14
  756.5 5.5 copy-start.15
  762.0 8.0 %copy-start.4 = (f32[136,816]{0,1:T(8,128)S(1)}, f32[136,816]{0,1:T(8,128)}, u32[]{:S(2)}) copy-start(f32[136,816]{0,1:T(8,128)} %get-tuple-element.190) | copy-start | bytes 1331716
  764.0 7.0 copy-start.17
  764.0 7.8 copy-start.3
  765.9 7.0 copy-start.16
  768.2 5.6 copy-start.26
  768.2 5.6 copy-start.27
  768.2 5.6 copy-start.28
Sparse Core Ops, SparseCore 0:
  13.0 39.5 all-gather.20
  58.3 38.0 all-gather.12
  98.6 55.5 all-gather.10
  159.4 52.7 all-gather.14
  238.4 34.9 all-gather.16
  275.4 30.5 all-gather.18
  314.3 27.5 reduce-scatter.40
  345.2 29.3 all-gather.22
  389.2 32.4 reduce-scatter.30
  423.8 36.0 reduce-scatter.28
  482.9 42.1 reduce-scatter.24
  527.3 31.2 reduce-scatter.26
  560.8 63.2 reduce-scatter.34
  626.3 55.0 reduce-scatter.32
  684.2 28.9 reduce-scatter.38
  719.7 33.6 reduce-scatter.36
where the time goes:
time: 794 us; the launch traced here: 781 us
  waiting for transfers between devices  434 us (55%)
  local copies, waits for them, and re-layouts  107 us (13%)
  blocking collectives  96.9 us (12%)
  matrix products  48.6 us (6%)
  Pallas kernels  34.4 us (4%)
  other arithmetic  26.7 us (3%)
  starting transfers between devices  17.8 us (2%)
  between operations  15.4 us (2%)
    all_gather x4, waiting for transfers between devices, gather_rows(): return lax.all_gather(rows, 'ctx', axis=0, tiled=True)  129 us
    unnamed x23, waiting for transfers between devices  110 us
    all_to_all x2, blocking collectives, exchange(): lax.all_to_all(blocks, 'ctx', split_axis=0, concat_axis=0, tiled=True)  72.6 us
    dot_general x12, matrix products, dot_on(): lax.dot_general(left, right, (((left_dim,), (right_dim,)), ((), ())), pre...  48.6 us
    unnamed x93, local copies, waits for them, and re-layouts  44.2 us
    all_gather x1, waiting for transfers between devices, local(): lax.all_gather(triple_t[feat:].reshape(2, feat, total), 'ctx', axis=0)  43.6 us
    all_gather x1, waiting for transfers between devices, local(): columns = lax.all_gather(packed, 'dp', axis=0)  39.7 us
    pallas_call x2, Pallas kernels, attention(): pl.pallas_call(kernel, grid=(H,), in_specs=[whole(query_pos), whole(key_p...  34.4 us
  transfers between devices with their start and end apart: 19, of which 14 were waited for; matrix products, arithmetic and copies ran while one was open for 14% of the time, Pallas kernels for 0%

commit v1 on v0

--- a/solution.py
+++ b/solution.py
@@ -131,7 +131,7 @@
     return lax.all_gather(rows, "ctx", axis=0, tiled=True)
 
 
-def local(
+def local_wide(
     inputs,
     out_grad,
     pair_blocks,
@@ -358,7 +358,790 @@
     )
 
 
+TILE = 2 * HD
+
+
+def peers_of(kinds):
+    me_c = lax.axis_index("ctx")
+    me_d = lax.axis_index("dp")
+    n = lax.axis_size("ctx")
+    m = lax.axis_size("dp")
+    chips = n // 2
+    chip = lax.div(me_c, 2)
+    core = lax.rem(me_c, 2)
+    found = []
+    if any(kind.endswith("dp") for kind in kinds):
+        found += [{"dp": lax.rem(me_d + r, m)} for r in range(1, m)]
+    if "swap_ctx" in kinds:
+        found += [{"ctx": lax.rem(me_c + r, n)} for r in range(1, n)]
+    elif any(kind.endswith("ctx") for kind in kinds):
+        found += [{"ctx": 2 * lax.rem(chip + r, chips) + core} for r in range(1, chips)]
+        found += [{"ctx": 2 * chip + 1 - core}]
+    return found
+
+
+def send(src, dst, send_sem, recv_sem, device):
+    return pltpu.make_async_remote_copy(
+        src_ref=src,
+        dst_ref=dst,
+        send_sem=send_sem,
+        recv_sem=recv_sem,
+        device_id=device,
+        device_id_type=pl.DeviceIdType.MESH,
+    )
+
+
+class GatherDp:
+    scratch = 0
+
+    def __init__(self, x, out, sems):
+        self.x, self.out, self.sems = x, out, sems
+        self.m = lax.axis_size("dp")
+        self.me = lax.axis_index("dp")
+
+    def piece(self, to):
+        return self.x
+
+    def target(self, of):
+        return self.out.at[of]
+
+    def copy(self, r, of, to):
+        return send(
+            self.piece(to),
+            self.target(of),
+            self.sems[0].at[r],
+            self.sems[1].at[of],
+            {"dp": to},
+        )
+
+    def start(self):
+        self.sent = []
+        for r in range(1, self.m):
+            copy = self.copy(r, self.me, lax.rem(self.me + r, self.m))
+            copy.start()
+            self.sent.append(copy)
+        self.keep()
+
+    def keep(self):
+        self.out[self.me] = self.x[...]
+
+    def middle(self):
+        pass
+
+    def finish(self):
+        for r in range(1, self.m):
+            of = lax.rem(self.me + self.m - r, self.m)
+            self.copy(r, of, of).wait_recv()
+        for copy in self.sent:
+            copy.wait_send()
+
+
+class SwapDp(GatherDp):
+    def piece(self, to):
+        return self.x.at[to]
+
+    def keep(self):
+        self.out[self.me] = self.x[self.me]
+
+
+class SumDp(SwapDp):
+    scratch = 1
+
+    def __init__(self, x, out, sems, got):
+        super().__init__(x, out, sems)
+        self.got = got
+
+    def target(self, of):
+        return self.got.at[of]
+
+    def keep(self):
+        pass
+
+    def finish(self):
+        super().finish()
+        total = self.x[self.me].astype(jnp.float32)
+        for r in range(1, self.m):
+            total = total + self.got[lax.rem(self.me + r, self.m)].astype(jnp.float32)
+        self.out[...] = total
+
+
+class SwapCtx(SwapDp):
+    def __init__(self, x, out, sems):
+        self.x, self.out, self.sems = x, out, sems
+        self.m = lax.axis_size("ctx")
+        self.me = lax.axis_index("ctx")
+
+    def copy(self, r, of, to):
+        return send(
+            self.piece(to),
+            self.target(of),
+            self.sems[0].at[r],
+            self.sems[1].at[of],
+            {"ctx": to},
+        )
+
+
+class GatherCtx:
+    scratch = 0
+
+    def __init__(self, x, out, sems):
+        self.x, self.out, self.sems = x, out, sems
+        self.chips = lax.axis_size("ctx") // 2
+        self.me = lax.axis_index("ctx")
+        self.chip = lax.div(self.me, 2)
+        self.core = lax.rem(self.me, 2)
+        self.partner = 2 * self.chip + 1 - self.core
+
+    def of_chip(self, r, core):
+        return 2 * lax.rem(self.chip + self.chips + r, self.chips) + core
+
+    def copy(self, src, slot, of, to):
+        return send(
+            src, self.out.at[of], self.sems[0].at[slot], self.sems[1].at[of], {"ctx": to}
+        )
+
+    def start(self):
+        self.sent = []
+        for r in range(1, self.chips):
+            copy = self.copy(self.x, r, self.me, self.of_chip(r, self.core))
+            copy.start()
+            self.sent.append(copy)
+        copy = self.copy(self.x, 0, self.me, self.partner)
+        copy.start()
+        self.sent.append(copy)
+        self.out[self.me] = self.x[...]
+
+    def middle(self):
+        for r in range(1, self.chips):
+            of = self.of_chip(-r, self.core)
+            self.copy(self.x, r, of, of).wait_recv()
+            copy = self.copy(self.out.at[of], self.chips + r, of, self.partner)
+            copy.start()
+            self.sent.append(copy)
+
+    def finish(self):
+        for r in range(self.chips):
+            of = self.of_chip(-r, 1 - self.core)
+            self.copy(self.x, 0, of, self.partner).wait_recv()
+        for copy in self.sent:
+            copy.wait_send()
+
+
+class SumCtx(GatherCtx):
+    scratch = 3
+
+    def __init__(self, x, out, sems, half, pre, got):
+        super().__init__(x, out, sems)
+        self.half, self.pre, self.got = half, pre, got
+
+    def early(self, r):
+        j = lax.rem(self.chip + r, self.chips)
+        return send(
+            self.x.at[2 * j + 1 - self.core],
+            self.half.at[j],
+            self.sems[0].at[r],
+            self.sems[1].at[j],
+            {"ctx": self.partner},
+        )
+
+    def late(self, r, of, to):
+        return send(
+            self.pre.at[to],
+            self.got.at[of],
+            self.sems[0].at[self.chips + r],
+            self.sems[1].at[self.chips + of],
+            {"ctx": 2 * to + self.core},
+        )
+
+    def start(self):
+        self.sent = []
+        for r in list(range(1, self.chips)) + [0]:
+            copy = self.early(r)
+            copy.start()
+            self.sent.append(copy)
+
+    def middle(self):
+        for r in range(1, self.chips):
+            self.early(r).wait_recv()
+            to = lax.rem(self.chip + r, self.chips)
+            total = self.x[2 * to + self.core].astype(jnp.float32) + self.half[to].astype(
+                jnp.float32
+            )
+            self.pre[to] = total.astype(self.pre.dtype)
+            copy = self.late(r, self.chip, to)
+            copy.start()
+            self.sent.append(copy)
+
+    def finish(self):
+        self.early(0).wait_recv()
+        total = self.x[self.me].astype(jnp.float32) + self.half[self.chip].astype(jnp.float32)
+        for r in range(1, self.chips):
+            of = lax.rem(self.chip + self.chips - r, self.chips)
+            self.late(r, of, of).wait_recv()
+            total = total + self.got[of].astype(jnp.float32)
+        self.out[...] = total
+        for copy in self.sent:
+            copy.wait_send()
+
+
+MOVES = {
+    "gather_dp": GatherDp,
+    "swap_dp": SwapDp,
+    "sum_dp": SumDp,
+    "gather_ctx": GatherCtx,
+    "swap_ctx": SwapCtx,
+    "sum_ctx": SumCtx,
+}
+
+
+def move_kernel(kinds, *refs):
+    count = len(kinds)
+    xs, outs, rest = refs[:count], refs[count : 2 * count], list(refs[2 * count :])
+    barrier = pltpu.get_barrier_semaphore()
+    peers = peers_of(kinds)
+    for peer in peers:
+        pl.semaphore_signal(
+            barrier, inc=1, device_id=peer, device_id_type=pl.DeviceIdType.MESH
+        )
+    pl.semaphore_wait(barrier, len(peers))
+    moves = []
+    for kind, x, out in zip(kinds, xs, outs):
+        sems = (rest.pop(0), rest.pop(0))
+        extra = [rest.pop(0) for _ in range(MOVES[kind].scratch)]
+        moves.append(MOVES[kind](x, out, sems, *extra))
+    for move in moves:
+        move.start()
+    for move in moves:
+        move.middle()
+    for move in moves:
+        move.finish()
+
+
+def move(collective_id, *pairs):
+    kinds = tuple(kind for kind, _ in pairs)
+    n = lax.axis_size("ctx")
+    m = lax.axis_size("dp")
+    shapes, scratch, sent = [], [], 0
+    for kind, x in pairs:
+        size = n if kind.endswith("ctx") else m
+        if kind.startswith("gather"):
+            shapes.append(jax.ShapeDtypeStruct((size,) + x.shape, x.dtype))
+            sent += (size - 1) * x.size * x.dtype.itemsize
+        elif kind.startswith("swap"):
+            shapes.append(jax.ShapeDtypeStruct(x.shape, x.dtype))
+            sent += x.size * x.dtype.itemsize
+        else:
+            shapes.append(jax.ShapeDtypeStruct(x.shape[1:], jnp.float32))
+            sent += x.size * x.dtype.itemsize
+        scratch += [pltpu.SemaphoreType.DMA((size,)), pltpu.SemaphoreType.DMA((size,))]
+        if kind == "sum_dp":
+            scratch += [pltpu.VMEM(x.shape, x.dtype)]
+        if kind == "sum_ctx":
+            scratch += [pltpu.VMEM((n // 2,) + x.shape[1:], x.dtype)] * 3
+    kernel = lambda *refs: move_kernel(kinds, *refs)
+    return pl.pallas_call(
+        kernel,
+        in_specs=[pl.BlockSpec(memory_space=pltpu.VMEM)] * len(kinds),
+        out_specs=[pl.BlockSpec(memory_space=pltpu.VMEM)] * len(kinds),
+        out_shape=shapes,
+        scratch_shapes=scratch,
+        compiler_params=pltpu.CompilerParams(
+            collective_id=collective_id, has_side_effects=True
+        ),
+        cost_estimate=pl.CostEstimate(flops=sent * 100, bytes_accessed=sent, transcendentals=0),
+        name="move_" + str(collective_id),
+    )(*[x for _, x in pairs])
+
+
+def pair_lanes(shape, half):
+    lane = lax.broadcasted_iota(jnp.int32, shape, 1)
+    return (lane < HD) if half == 0 else (lane >= HD)
+
+
+def causal(shape):
+    row = lax.broadcasted_iota(jnp.int32, shape, 0)
+    return row >= lax.broadcasted_iota(jnp.int32, shape, 1)
+
+
+def sort_rows(order_ref, src, dst):
+    for b in range(src.shape[0] // BLK):
+        start = pl.multiple_of(order_ref[b] * BLK, BLK)
+        dst[b * BLK : (b + 1) * BLK, :] = src[pl.ds(start, BLK), :]
+
+
+def unsort_rows(order_ref, src, dst):
+    for b in range(dst.shape[0] // BLK):
+        start = pl.multiple_of(order_ref[b] * BLK, BLK)
+        dst[pl.ds(start, BLK), :] = src[b * BLK : (b + 1) * BLK, :]
+
+
+def head_slots():
+    return ((0, 0), (0, 1), (1, 0))
+
+
+def pairs_forward(order_ref, qkv_ref, out_ref, log_ref, rows, outs):
+    sort_rows(order_ref, qkv_ref, rows)
+    seq = qkv_ref.shape[0]
+    step = min(4 * BLK, seq)
+    for i in range(seq // step):
+        at = slice(i * step, (i + 1) * step)
+        results, logs = [], []
+        for block, half in head_slots():
+            lanes = lambda part: slice((2 * part + block) * TILE, (2 * part + block + 1) * TILE)
+            query = rows[at, lanes(0)] * HD ** (-0.5)
+            query = query.astype(jnp.bfloat16)
+            if block == 0:
+                query = jnp.where(pair_lanes(query.shape, half), query, jnp.zeros_like(query))
+            last = dot_on(query, rows[at, lanes(1)], 1, 1)
+            last = jnp.where(causal(last.shape), last, masked_score)
+            top = jnp.max(last, axis=1, keepdims=True)
+            if i > 0:
+                early = dot_on(query, rows[: i * step, lanes(1)], 1, 1)
+                top = jnp.maximum(top, jnp.max(early, axis=1, keepdims=True))
+            last = jnp.exp(last - top)
+            total = jnp.sum(last, axis=1, keepdims=True)
+            if i > 0:
+                early = jnp.exp(early - top)
+                total = total + jnp.sum(early, axis=1, keepdims=True)
+            scale = 1.0 / total
+            result = dot_on((last * scale).astype(jnp.bfloat16), rows[at, lanes(2)], 1, 0)
+            if i > 0:
+                result = result + dot_on(
+                    (early * scale).astype(jnp.bfloat16), rows[: i * step, lanes(2)], 1, 0
+                )
+            results.append(result)
+            logs.append(top + jnp.log(total))
+        first = pair_lanes((step, TILE), 0)
+        outs[at, :TILE] = jnp.where(first, results[0], results[1]).astype(jnp.bfloat16)
+        outs[at, TILE:] = results[2].astype(jnp.bfloat16)
+        lane = lax.broadcasted_iota(jnp.int32, (step, TILE), 1)
+        log_ref[at, :] = jnp.where(lane == 0, logs[0], jnp.where(lane == 1, logs[1], logs[2]))
+    unsort_rows(order_ref, outs, out_ref)
+
+
+def pairs_backward(
+    order_ref, qkv_ref, out_ref, log_ref, dout_ref, dqkv_ref, rows, outs, douts, grads, dkey, dvalue
+):
+    sort_rows(order_ref, qkv_ref, rows)
+    sort_rows(order_ref, out_ref, outs)
+    sort_rows(order_ref, dout_ref, douts)
+    seq = qkv_ref.shape[0]
+    step = min(4 * BLK, seq)
+    dkey[...] = jnp.zeros_like(dkey)
+    dvalue[...] = jnp.zeros_like(dvalue)
+    for i in range(seq // step):
+        at = slice(i * step, (i + 1) * step)
+        dqueries = []
+        for slot, (block, half) in enumerate(head_slots()):
+            lanes = lambda part: slice((2 * part + block) * TILE, (2 * part + block + 1) * TILE)
+            own = slice(block * TILE, (block + 1) * TILE)
+            query = (rows[at, lanes(0)] * HD ** (-0.5)).astype(jnp.bfloat16)
+            dout = douts[at, own]
+            if block == 0:
+                mask = pair_lanes(query.shape, half)
+                query = jnp.where(mask, query, jnp.zeros_like(query))
+                dout = jnp.where(mask, dout, jnp.zeros_like(dout))
+            delta = jnp.sum(
+                dout.astype(jnp.float32) * outs[at, own].astype(jnp.float32), axis=1, keepdims=True
+            )
+            log_total = log_ref[at, slot : slot + 1]
+            dquery = None
+            for keys, diagonal in ((at, True), (slice(0, i * step), False)):
+                if keys.stop == 0:
+                    continue
+                scores = dot_on(query, rows[keys, lanes(1)], 1, 1)
+                probs = jnp.exp(scores - log_total)
+                if diagonal:
+                    probs = jnp.where(causal(probs.shape), probs, 0.0)
+                dprobs = dot_on(dout, rows[keys, lanes(2)], 1, 1)
+                dscores = (probs * (dprobs - delta)).astype(jnp.bfloat16)
+                part = dot_on(dscores, rows[keys, lanes(1)], 1, 0)
+                dquery = part if dquery is None else dquery + part
+                dkey[own, keys] += dot_on(query, dscores, 0, 0)
+                dvalue[own, keys] += dot_on(dout, probs.astype(jnp.bfloat16), 0, 0)
+            dqueries.append(dquery * HD ** (-0.5))
+        first = pair_lanes((step, TILE), 0)
+        grads[at, :TILE] = jnp.where(first, dqueries[0], dqueries[1]).astype(jnp.bfloat16)
+        third = jnp.where(first, dqueries[2], 0.0)
+        grads[at, TILE : 2 * TILE] = third.astype(jnp.bfloat16)
+    for block in range(2):
+        own = slice(block * TILE, (block + 1) * TILE)
+        grads[:, (2 + block) * TILE : (3 + block) * TILE] = dkey[own, :].T.astype(jnp.bfloat16)
+        grads[:, (4 + block) * TILE : (5 + block) * TILE] = dvalue[own, :].T.astype(jnp.bfloat16)
+    unsort_rows(order_ref, grads, dqkv_ref)
+
+
+def attend(kernel, order, arrays, shapes, scratch, matmuls):
+    seq = arrays[0].shape[0]
+    vmem = pl.BlockSpec(memory_space=pltpu.VMEM)
+    return pl.pallas_call(
+        kernel,
+        in_specs=[pl.BlockSpec(memory_space=pltpu.SMEM)] + [vmem] * len(arrays),
+        out_specs=[vmem] * len(shapes),
+        out_shape=shapes,
+        scratch_shapes=scratch,
+        cost_estimate=pl.CostEstimate(
+            flops=3 * matmuls * seq * seq * TILE,
+            bytes_accessed=seq * 24 * TILE,
+            transcendentals=2 * seq * seq,
+        ),
+    )(order, *arrays)
+
+
+def turn(x, r):
+    n = lax.axis_size("ctx")
+    chips = n // 2
+    pairs = [(2 * q + k, 2 * ((q + r) % chips) + k) for q in range(chips) for k in range(2)]
+    return lax.ppermute(x, "ctx", pairs)
+
+
+def trade(x):
+    return lax.ppermute(x, "ctx", [(c, c ^ 1) for c in range(lax.axis_size("ctx"))])
+
+
+def line_gather(x):
+    chips = lax.axis_size("ctx") // 2
+    chip = lax.axis_index("ctx") // 2
+    out = jnp.zeros((chips,) + x.shape, x.dtype)
+    for r in range(chips):
+        piece = x if r == 0 else turn(x, r)
+        out = lax.dynamic_update_index_in_dim(out, piece, (chip - r) % chips, 0)
+    return out
+
+
+def line_sum(x):
+    chips = lax.axis_size("ctx") // 2
+    chip = lax.axis_index("ctx") // 2
+    total = lax.dynamic_index_in_dim(x, chip, 0, False).astype(jnp.float32)
+    for r in range(1, chips):
+        piece = lax.dynamic_index_in_dim(x, (chip + r) % chips, 0, False)
+        total = total + turn(piece, r).astype(jnp.float32)
+    return total
+
+
+def both_cores(x, other, axis):
+    core = lax.axis_index("ctx") % 2
+    return jnp.where(core == 0, jnp.stack([x, other], axis), jnp.stack([other, x], axis))
+
+
+def core_sum(x, axis):
+    core = lax.axis_index("ctx") % 2
+    mine = lax.dynamic_index_in_dim(x, core, axis, False)
+    other = lax.dynamic_index_in_dim(x, 1 - core, axis, False)
+    return (mine.astype(jnp.float32) + trade(other).astype(jnp.float32)).astype(x.dtype)
+
+
+def swap_dp(x):
+    m = lax.axis_size("dp")
+    me = lax.axis_index("dp")
+    out = jnp.zeros_like(x)
+    for r in range(m):
+        piece = lax.dynamic_index_in_dim(x, (me + r) % m, 0, False)
+        if r:
+            piece = lax.ppermute(piece, "dp", [(d, (d + r) % m) for d in range(m)])
+        out = lax.dynamic_update_index_in_dim(out, piece, (me - r) % m, 0)
+    return out
+
+
+def local_pairs(
+    inputs,
+    out_grad,
+    pair_blocks,
+    triple_weight,
+    merge_weight,
+    expand_weight,
+    shrink_weight,
+    vector_params,
+    triple_moment,
+    merge_moment,
+    expand_moment,
+    shrink_moment,
+    vector_moment,
+    triple_square,
+    merge_square,
+    expand_square,
+    shrink_square,
+    vector_square,
+):
+    bf16 = jnp.bfloat16
+    f32 = jnp.float32
+    n = lax.axis_size("ctx")
+    m = lax.axis_size("dp")
+    here = lax.axis_index("ctx")
+    seq_here = lax.axis_index("dp")
+    chips = n // 2
+    rows = inputs.shape[1]
+    total = rows * n
+    feat = D // n
+    cut = n * TILE
+    spare = D - cut
+    wide = expand_weight.shape[1]
+    hid = shrink_weight.shape[0]
+    fold = wide // hid
+    cols = shrink_weight.shape[1]
+    stream = inputs[0]
+    cotangent = out_grad[0]
+    tw, mw = triple_weight.shape[1], merge_weight.shape[1]
+
+    flat = pair_blocks.reshape(-1)
+    blocks = jnp.arange(flat.shape[0], dtype=jnp.int32)
+    order = jnp.sum(jnp.where(flat[None, :] == blocks[:, None], blocks[None, :], 0), axis=1)
+
+    w_expand_own = expand_weight.astype(bf16)
+    w_shrink_own = (
+        shrink_weight.astype(bf16)
+        .T.reshape(fold, cols // fold, hid)
+        .transpose(1, 0, 2)
+        .reshape(cols // fold, wide)
+    )
+    packed = jnp.concatenate(
+        [triple_weight.astype(bf16), merge_weight.astype(bf16), vector_params.astype(bf16)], axis=1
+    )
+    normed_one, inverse_one = layer_norm(stream)
+    cot_b = cotangent.astype(bf16)
+    normed_full, columns, cot_full = move(
+        0, ("gather_ctx", normed_one.astype(bf16)), ("gather_dp", packed), ("gather_dp", cot_b)
+    )
+    normed_full = normed_full.reshape(total, D)
+    cot_full = cot_full.reshape(m * rows, D)
+
+    expand_line = line_gather(w_expand_own)
+    w_expand = both_cores(expand_line, trade(expand_line), 1).reshape(D, wide)
+    shrink_line = swap_dp(line_gather(w_shrink_own))
+    w_shrink_t = (
+        both_cores(shrink_line, trade(shrink_line), 1)
+        .reshape(m, fold, cols // fold, fold, hid)
+        .transpose(0, 3, 2, 1, 4)
+        .reshape(D, wide)
+    )
+
+    def take(start, width):
+        return columns[:, :, start : start + width].transpose(1, 0, 2).reshape(feat, m * width)
+
+    triple_rows = take(0, tw).reshape(feat, 3, D)
+    merge_rows = take(tw, mw)
+    vector_rows = take(tw + mw, vector_params.shape[1])
+    slabs = (
+        triple_rows[:, :, :cut].reshape(feat, 3, n, TILE).transpose(2, 0, 1, 3).reshape(n, feat, -1)
+    )
+    common = jnp.concatenate([triple_rows[:, :, cut:].reshape(feat, 3 * spare), vector_rows], axis=1)
+    w_main, w_common = move(1, ("swap_ctx", slabs), ("gather_ctx", common))
+    merge_line = line_gather(merge_rows)
+    w_merge = both_cores(merge_line, trade(merge_line), 1).reshape(D, D)
+    w_main = w_main.reshape(D, 3, TILE)
+    w_common = w_common.reshape(D, -1)
+    w_last = w_common[:, : 3 * spare].reshape(D, 3, spare)
+    w_last = jnp.pad(w_last, ((0, 0), (0, 0), (0, TILE - spare)))
+    w_triple = jnp.concatenate([w_main, w_last], axis=2).reshape(D, 6 * TILE)
+    vectors = w_common[:, 3 * spare :].astype(f32)
+    gain_one = vectors[:, 0]
+    shift_one = vectors[:, 1]
+    merge_bias = vectors[:, 4]
+    gain_two = vectors[:, 5]
+    shift_two = vectors[:, 6]
+    shrink_bias = vectors[:, 7]
+    expand_bias = lax.dynamic_slice_in_dim(vectors[:, 8:].T.reshape(-1), seq_here * wide, wide)
+
+    def own_bias(column):
+        main = lax.dynamic_slice_in_dim(vectors[:, column], here * TILE, TILE)
+        last = jnp.pad(vectors[cut:, column], (0, TILE - spare))
+        return jnp.concatenate([main, last])
+
+    zeros = jnp.zeros((2 * TILE,), f32)
+    bias = jnp.concatenate([own_bias(2), zeros, own_bias(3)])
+    act_one = (normed_full.astype(f32) * gain_one + shift_one).astype(bf16)
+    qkv = (dot_on(act_one, w_triple, 1, 0) + bias).astype(bf16)
+    rows_scratch = pltpu.VMEM((total, 6 * TILE), bf16)
+    half_scratch = pltpu.VMEM((total, 2 * TILE), bf16)
+    attended, log_total = attend(
+        pairs_forward,
+        order,
+        (qkv,),
+        [
+            jax.ShapeDtypeStruct((total, 2 * TILE), bf16),
+            jax.ShapeDtypeStruct((total, TILE), f32),
+        ],
+        [rows_scratch, half_scratch],
+        2,
+    )
+    (att_main,) = move(2, ("swap_ctx", attended[:, :TILE].reshape(n, rows, TILE)))
+    att_last = lax.dynamic_slice(attended, (here * rows, TILE), (rows, spare))
+    att_own = jnp.concatenate(
+        [att_main.transpose(1, 0, 2).reshape(rows, cut), att_last], axis=1
+    )
+    middle = stream + dot_on(att_own, w_merge, 1, 0) + merge_bias
+    normed_two, inverse_two = layer_norm(middle)
+    (act_two,) = move(3, ("gather_dp", (normed_two * gain_two + shift_two).astype(bf16)))
+    act_two = act_two.reshape(m * rows, D)
+    pre_act = dot_on(act_two, w_expand, 1, 0) + expand_bias
+    hidden_b = gelu_value(pre_act).astype(bf16)
+    dpre = dot_on(cot_full, w_shrink_t, 1, 0) * gelu_slope(pre_act)
+    dpre_b = dpre.astype(bf16)
+    expand_bias_grad = jnp.sum(dpre, axis=0)
+    dact_part = dot_on(dpre_b, w_expand, 1, 1).astype(bf16).reshape(m, rows, D)
+    (dact_two,) = move(4, ("sum_dp", dact_part))
+    out_part = dot_on(hidden_b, w_shrink_t, 1, 1).astype(bf16).reshape(m, rows, D)
+
+    expand_part = dot_on(act_two, dpre_b, 0, 0).astype(bf16).reshape(chips, 2, feat, wide)
+    expand_grad = line_sum(core_sum(expand_part, 1))
+    shrink_part = (
+        dot_on(cot_full, hidden_b, 0, 0)
+        .astype(bf16)
+        .reshape(m, fold, cols // fold, fold, hid)
+        .transpose(0, 3, 2, 1, 4)
+        .reshape(m, fold, cols // fold, wide)
+    )
+    shrink_own = line_sum(swap_dp(core_sum(shrink_part, 1)))
+    shrink_grad = (
+        shrink_own.reshape(cols // fold, fold, hid).transpose(1, 0, 2).reshape(cols, hid).T
+    )
+
+    shrink_bias_grad = jnp.sum(cotangent, axis=0)
+    gain_two_grad = jnp.sum(dact_two * normed_two, axis=0)
+    shift_two_grad = jnp.sum(dact_two, axis=0)
+    dmiddle = cotangent + norm_back(dact_two, normed_two, inverse_two, gain_two)
+    dmiddle_b = dmiddle.astype(bf16)
+    merge_bias_grad = jnp.sum(dmiddle, axis=0)
+    dattended = dot_on(dmiddle_b, w_merge, 1, 1).astype(bf16)
+    datt_main, datt_last = move(
+        5,
+        ("swap_ctx", dattended[:, :cut].reshape(rows, n, TILE).transpose(1, 0, 2)),
+        ("gather_ctx", jnp.pad(dattended[:, cut:], ((0, 0), (0, TILE - spare)))),
+    )
+    merge_part = dot_on(att_own, dmiddle_b, 0, 0).astype(bf16).reshape(chips, 2, feat, D)
+    merge_rows_grad = line_sum(core_sum(merge_part, 1))
+    datt = jnp.concatenate(
+        [datt_main.reshape(total, TILE), datt_last.reshape(total, TILE)], axis=1
+    )
+    (dqkv,) = attend(
+        pairs_backward,
+        order,
+        (qkv, attended, log_total, datt),
+        [jax.ShapeDtypeStruct((total, 6 * TILE), bf16)],
+        [
+            rows_scratch,
+            half_scratch,
+            half_scratch,
+            rows_scratch,
+            pltpu.VMEM((2 * TILE, total), f32),
+            pltpu.VMEM((2 * TILE, total), f32),
+        ],
+        5,
+    )
+    lane = lax.broadcasted_iota(jnp.int32, (1, 6 * TILE), 1)
+    counted = ((lane // TILE) % 2 == 0) | (here == 0)
+    w_counted = jnp.where(counted, w_triple, jnp.zeros_like(w_triple))
+    dact_part = dot_on(dqkv, w_counted, 1, 1).astype(bf16).reshape(n, rows, D)
+    dact_one, out_sum = move(6, ("sum_ctx", dact_part), ("sum_dp", out_part))
+    block_out = middle + out_sum + shrink_bias
+    bias_grads = jnp.where(counted[0], jnp.sum(dqkv.astype(f32), axis=0), 0.0)
+    gain_one_grad = jnp.sum(dact_one * normed_one, axis=0)
+    shift_one_grad = jnp.sum(dact_one, axis=0)
+    input_rows = dmiddle + norm_back(dact_one, normed_one, inverse_one, gain_one)
+
+    def place(part):
+        main = lax.dynamic_update_slice_in_dim(
+            jnp.zeros((cut,), f32), bias_grads[2 * part * TILE :][:TILE], here * TILE, 0
+        )
+        return jnp.concatenate([main, bias_grads[(2 * part + 1) * TILE :][:spare]])
+
+    expand_bias_all = lax.dynamic_update_slice_in_dim(
+        jnp.zeros((m * wide,), f32), expand_bias_grad, seq_here * wide, 0
+    )
+    vector_local = jnp.concatenate(
+        [
+            jnp.stack(
+                [
+                    gain_one_grad,
+                    shift_one_grad,
+                    place(0),
+                    place(2),
+                    merge_bias_grad,
+                    gain_two_grad,
+                    shift_two_grad,
+                    shrink_bias_grad,
+                ],
+                axis=1,
+            ),
+            expand_bias_all.reshape(-1, D).T,
+        ],
+        axis=1,
+    )
+    triple_part = dot_on(act_one, dqkv, 0, 0).astype(bf16).reshape(D, 3, 2, TILE)
+    triple_main, vector_rows_grad = move(
+        7,
+        ("swap_ctx", triple_part[:, :, 0].reshape(n, feat, 3 * TILE)),
+        ("sum_ctx", vector_local.reshape(n, feat, -1)),
+    )
+    triple_last = lax.dynamic_slice_in_dim(triple_part[:, :, 1, :spare], here * feat, feat, 0)
+    triple_rows_grad = jnp.concatenate(
+        [
+            triple_main.reshape(n, feat, 3, TILE).transpose(1, 2, 0, 3).reshape(feat, 3, cut),
+            triple_last,
+        ],
+        axis=2,
+    )
+
+    def by_dp(rows_part):
+        return rows_part.reshape(feat, m, -1).transpose(1, 0, 2).astype(bf16)
+
+    (last,) = move(
+        8,
+        (
+            "sum_dp",
+            jnp.concatenate(
+                [by_dp(triple_rows_grad), by_dp(merge_rows_grad), by_dp(vector_rows_grad)], axis=2
+            ),
+        ),
+    )
+    triple_grad = last[:, :tw]
+    merge_grad = last[:, tw : tw + mw]
+    vector_grad = last[:, tw + mw :]
+    triple_new, triple_moment_new, triple_square_new = adam_update(
+        triple_weight, triple_grad, triple_moment, triple_square, True
+    )
+    merge_new, merge_moment_new, merge_square_new = adam_update(
+        merge_weight, merge_grad, merge_moment, merge_square, True
+    )
+    expand_new, expand_moment_new, expand_square_new = adam_update(
+        expand_weight, expand_grad, expand_moment, expand_square, True
+    )
+    shrink_new, shrink_moment_new, shrink_square_new = adam_update(
+        shrink_weight, shrink_grad, shrink_moment, shrink_square, True
+    )
+    vector_new, vector_moment_new, vector_square_new = adam_update(
+        vector_params, vector_grad, vector_moment, vector_square, False
+    )
+    return (
+        block_out[None],
+        input_rows[None],
+        triple_grad,
+        merge_grad,
+        expand_grad,
+        shrink_grad,
+        vector_grad,
+        triple_new,
+        merge_new,
+        expand_new,
+        shrink_new,
+        vector_new,
+        triple_moment_new,
+        merge_moment_new,
+        expand_moment_new,
+        shrink_moment_new,
+        vector_moment_new,
+        triple_square_new,
+        merge_square_new,
+        expand_square_new,
+        shrink_square_new,
+        vector_square_new,
+    )
+
+
 def solution(mesh):
+    heads = H // 2
+    even = mesh.shape["ctx"] == heads == 2 * mesh.shape["dp"]
+    local = local_pairs if even else local_wide
     in_specs = (
         P("dp", "ctx", None),
         P("dp", "ctx", None),

time: 794 us -> 676 us (0.85)
  waiting for transfers between devices: 434 us -> 110 us
  Pallas kernels: 34.4 us -> 259 us
  blocking collectives: 96.9 us -> 0 us
  local copies, waits for them, and re-layouts: 107 us -> 164 us
  other arithmetic: 26.7 us -> 65.8 us
  between operations: 15.4 us -> 2.15 us
  matrix products: 48.6 us -> 37.2 us
  starting transfers between devices: 17.8 us -> 28.9 us
    all_gather x7 -> x0, waiting for transfers between devices: 242 us -> none  [the longest x4 129 us: gather_rows(): return lax.all_gather(rows, 'ctx', axis=0, tiled=True)]
    pallas_call x2 -> x11, Pallas kernels: 34.4 us -> 259 us  [the longest x9 241 us: move(): pl.pallas_call(kernel, in_specs=[pl.BlockSpec(memory_space=pltpu.VMEM)] *...]
    unnamed x23 -> x0, waiting for transfers between devices: 110 us -> none
    ppermute x0 -> x30, waiting for transfers between devices: none -> 110 us  [the longest x18 85.3 us: turn(): return lax.ppermute(x, 'ctx', pairs)]
    all_to_all x2 -> x0, blocking collectives: 72.6 us -> none  [exchange(): lax.all_to_all(blocks, 'ctx', split_axis=0, concat_axis=0, tiled=True)]
    reduce_scatter x2 -> x0, waiting for transfers between devices: 50.2 us -> none  [the longest x1 32.4 us: local(): lax.psum_scatter(dvalue_t, 'ctx', scatter_dimension=0, tiled=True)]
    reshape x6 -> x19, local copies, waits for them, and re-layouts: 10 us -> 46.5 us  [the longest x3 19.2 us: local_pairs(): shrink_part = dot_on(cot_full, hidden_b, 0, 0).astype(bf16).reshape(m, fo...]
    all_to_all x3 -> x0, waiting for transfers between devices: 32.5 us -> none  [exchange(): lax.all_to_all(blocks, 'ctx', split_axis=0, concat_axis=0, tiled=True)]
  transfers between devices with their start and end apart: 19 -> 30, of which waited for: 14 -> 13; matrix products, arithmetic and copies ran while one was open for 14% -> 18% of each run, Pallas kernels for 0% -> 26%
where the time goes in v1:
time: 676 us; the launch traced here: 666 us
  Pallas kernels  259 us (38%)
  local copies, waits for them, and re-layouts  164 us (24%)
  waiting for transfers between devices  110 us (16%)
  other arithmetic  65.8 us (10%)
  matrix products  37.2 us (6%)
  starting transfers between devices  28.9 us (4%)
    pallas_call x9, Pallas kernels, move(): pl.pallas_call(kernel, in_specs=[pl.BlockSpec(memory_space=pltpu.VMEM)] *...  241 us
    ppermute x18, waiting for transfers between devices, turn(): return lax.ppermute(x, 'ctx', pairs)  85.3 us
    dot_general x12, matrix products, dot_on(): lax.dot_general(left, right, (((left_dim,), (right_dim,)), ((), ())), pre...  37.2 us
    ppermute x6, waiting for transfers between devices, swap_dp(): piece = lax.ppermute(piece, 'dp', [(d, (d + r) % m) for d in range(m)])  21.4 us
    reshape x3, local copies, waits for them, and re-layouts, local_pairs(): shrink_part = dot_on(cot_full, hidden_b, 0, 0).astype(bf16).reshape(m, fo...  19.2 us
    ppermute x18, starting transfers between devices, turn(): return lax.ppermute(x, 'ctx', pairs)  18.8 us
    pallas_call x2, Pallas kernels, attend(): pl.pallas_call(kernel, in_specs=[pl.BlockSpec(memory_space=pltpu.SMEM)] +...  17.8 us
    another operation x4, local copies, waits for them, and re-layouts, both_cores(): jnp.stack([x, other], axis)  17.3 us
  transfers between devices with their start and end apart: 30, of which 13 were waited for; matrix products, arithmetic and copies ran while one was open for 18% of the time, Pallas kernels for 26%

profile of v1, /device:TPU:9, one launch (start us, length us, event | category | flops | bytes accessed | tf_op | source)
XLA Modules:
  0.0 666.3 jit_solution(6578342483802538985)
XLA Ops:
  6.5 35.2 %move_0.1 = (bf16[8,128,1088]{2,1,0:T(8,128)(2,1)}, bf16[4,136,1091]{2,1,0:T(8,128)(2,1)}, bf16[4,128,1088]{2,1,0:T(8,128)(2,1)}) custom-call(bf16[128,1088]{1,0:T(8,128)(2,1)} %fusion.30.refs_0_, bf16[136,1091]{1,0:T(8,128)(2,1)} %concatenate.54.refs_1_, bf16[128,1088]{1,0:T(8,128)(2,1)} %bitcast_convert_fusion.refs_2_), custom_call_target="tpu_custom_call" | custom-call | flops 367553600 | bytes 3675536 | tf_op jit(solution)/shard_map/move_0/pallas_call | solution.py:642
  49.4 2.5 collective-permute-start.12
  63.8 56.8 %move_1.1 = (bf16[8,136,384]{2,1,0:T(8,128)(2,1)}, bf16[8,136,204]{2,1,0:T(8,128)(2,1)}) custom-call(bf16[8,136,384]{2,1,0:T(8,128)(2,1)} %reshape.337.refs_0_, bf16[136,204]{1,0:T(8,128)(2,1)} %pad_maximum_fusion.5.refs_1_), custom_call_target="tpu_custom_call" | custom-call | flops 122400000 | bytes 1224000 | tf_op jit(solution)/shard_map/move_1/pallas_call | solution.py:642
  125.3 2.5 reshape.341
  127.8 2.4 fusion.13
  130.2 5.4 copy.327
  137.9 3.4 add_convert_fusion.1.qkv_ref
  141.4 7.9 %shard_map.345 = (bf16[1024,256]{1,0:T(8,128)(2,1)}, f32[1024,128]{1,0:T(8,128)}) custom-call(s32[16]{0:T(128)} %select_reduce_fusion.order_ref, bf16[1024,768]{1,0:T(8,128)(2,1)} %add_convert_fusion.1.qkv_ref), custom_call_target="tpu_custom_call" | custom-call | flops 805306368 | bytes 3145728 | tf_op jit(solution)/shard_map/pallas_call | solution.py:777
  152.2 9.9 %move_2.1 = bf16[8,128,128]{2,1,0:T(8,128)(2,1)} custom-call(bf16[8,128,128]{2,1,0:T(8,128)(2,1)} %bitcast.264), custom_call_target="tpu_custom_call" | custom-call | flops 26214400 | bytes 262144 | tf_op jit(solution)/shard_map/move_2/pallas_call | solution.py:642
  177.8 18.3 %move_3.1 = bf16[4,128,1088]{2,1,0:T(8,128)(2,1)} custom-call(bf16[128,1088]{1,0:T(8,128)(2,1)} %add_convert_fusion.2.refs_0_), custom_call_target="tpu_custom_call" | custom-call | flops 83558400 | bytes 835584 | tf_op jit(solution)/shard_map/move_3/pallas_call | solution.py:642
  196.1 2.9 maximum_select_fusion.1
  203.6 3.3 convolution_convert_fusion
  206.9 7.2 %reshape.366 = bf16[4,2,136,2,544]{4,3,2,1,0:T(2,128)(2,1)} reshape(bf16[1088,1088]{1,0:T(8,128)(2,1)} %convolution_convert_fusion) | data formatting | bytes 4734976 | tf_op jit(solution)/shard_map/reshape | solution.py:990
  214.1 5.5 copy.390
  219.6 6.6 reshape.367
  226.2 2.5 dynamic-slice_bitcast_fusion
  229.2 2.9 collective-permute-done.23
  239.7 6.3 collective-permute-done.24
  247.7 5.6 collective-permute-done.25
  256.9 2.9 collective-permute-start.28
  261.3 4.3 collective-permute-done.27
  265.6 18.2 %collective-permute-done.28 = bf16[136,1088]{1,0:T(8,128)(2,1)} collective-permute-done((bf16[136,1088]{1,0:T(8,128)(2,1)}, bf16[136,1088]{1,0:T(8,128)(2,1)}, u32[]{:S(2)}, u32[]{:S(2)}) %collective-permute-start.28) | collective-permute-done | bytes 295968 | tf_op jit(solution)/shard_map/ppermute | solution.py:795
  283.8 4.4 collective-permute-done.29
  290.3 2.4 reshape.368
  293.9 3.6 multiply_subtract_fusion
  302.3 5.2 collective-permute-done.4
  308.5 17.2 %collective-permute-done.5 = bf16[136,1088]{1,0:T(8,128)(2,1)S(1)} collective-permute-done((bf16[136,1088]{1,0:T(8,128)(2,1)}, bf16[136,1088]{1,0:T(8,128)(2,1)S(1)}, u32[]{:S(2)}, u32[]{:S(2)}) %collective-permute-start.5) | collective-permute-done | bytes 295968 | tf_op jit(solution)/shard_map/ppermute | solution.py:795
  331.2 2.7 collective-permute-start.9
  334.0 3.2 collective-permute-done.7
  338.9 6.3 collective-permute-done.8
  348.6 3.7 fusion.1
  352.4 4.3 stack.54
  356.7 5.0 copy.335
  361.7 4.3 stack.55
  366.0 3.6 copy.336
  369.7 15.3 %fusion.3 = bf16[4,2,136,2,544]{4,3,2,1,0:T(2,128)(2,1)} fusion(pred[]{:T(512)S(6)} %eq.83, bf16[4,1,136,2,544]{4,1,2,3,0:T(2,128)(2,1)S(1)} %copy.336, bf16[4,1,136,2,544]{4,1,2,3,0:T(2,128)(2,1)S(1)} %copy-done.2), kind=kLoop, calls=%fused_computation.20 | loop fusion | flops 10653696 | bytes 4734977 | tf_op jit(solution)/shard_map/transpose | solution.py:914
  385.0 6.8 %reshape.350 = bf16[1088,1088]{1,0:T(8,128)(2,1)} reshape(bf16[4,2,136,2,544]{4,3,2,1,0:T(2,128)(2,1)} %fusion.3) | data formatting | bytes 4734976 | tf_op jit(solution)/shard_map/reshape | solution.py:915
  391.7 6.3 fusion.56
  398.1 3.2 convolution_convert_fusion.1
  401.3 2.6 convolution_convert_fusion.6
  403.9 2.4 copy.340
  406.2 20.9 %move_4.1 = f32[128,1088]{1,0:T(8,128)} custom-call(bf16[4,128,1088]{2,1,0:T(8,128)(2,1)} %bitcast.239), custom_call_target="tpu_custom_call" | custom-call | flops 111411200 | bytes 1114112 | tf_op jit(solution)/shard_map/move_4/pallas_call | solution.py:642
  430.4 2.3 convolution_convert_fusion.2
  434.4 2.8 convolution_convert_fusion.5
  437.8 16.3 %move_5.1 = (bf16[8,128,128]{2,1,0:T(8,128)(2,1)}, bf16[8,128,128]{2,1,0:T(8,128)(2,1)}) custom-call(bf16[8,128,128]{2,1,0:T(8,128)(2,1)} %bitcast_bitcast_fusion.refs_0_, bf16[128,128]{1,0:T(8,128)(2,1)} %pad.18.refs_1_), custom_call_target="tpu_custom_call" | custom-call | flops 49152000 | bytes 491520 | tf_op jit(solution)/shard_map/move_5/pallas_call | solution.py:642
  456.0 9.9 %shard_map.346 = bf16[1024,768]{1,0:T(8,128)(2,1)} custom-call(s32[16]{0:T(128)} %select_reduce_fusion.order_ref, bf16[1024,768]{1,0:T(8,128)(2,1)} %add_convert_fusion.1.qkv_ref, bf16[1024,256]{1,0:T(8,128)(2,1)} %get-tuple-element.39.out_ref, f32[1024,128]{1,0:T(8,128)} %get-tuple-element.40.log_ref, bf16[1024,256]{1,0:T(8,128)(2,1)} %pad_maximum_fusion.1.dout_ref), custom_call_target="tpu_custom_call" | custom-call | flops 2013265920 | bytes 3145728 | tf_op jit(solution)/shard_map/pallas_call | solution.py:777
  467.6 5.0 convolution_convert_fusion.4
  472.6 3.5 reshape.359
  476.1 7.0 %slice_reduce_fusion = bf16[1088,3,128]{2,1,0:T(4,128)(2,1)S(1)} fusion(bf16[1088,3,2,128]{3,2,1,0:T(2,128)(2,1)S(1)} %reshape.359), kind=kLoop, calls=%fused_computation.42 | loop fusion | bytes 1671168 | tf_op jit(solution)/shard_map/slice | solution.py:1073
  483.1 2.8 slice.144
  489.1 2.6 copy.344
  491.6 5.0 convolution_convert_fusion.3
  496.6 4.2 copy.343
  500.8 34.2 %move_6.1 = (f32[128,1088]{1,0:T(8,128)}, f32[128,1088]{1,0:T(8,128)}) custom-call(bf16[8,128,1088]{2,1,0:T(8,128)(2,1)} %bitcast.236, bf16[4,128,1088]{2,1,0:T(8,128)(2,1)} %bitcast.238), custom_call_target="tpu_custom_call" | custom-call | flops 334233600 | bytes 3342336 | tf_op jit(solution)/shard_map/move_6/pallas_call | solution.py:642
  540.6 29.8 %move_7.1 = (bf16[8,136,384]{2,1,0:T(8,128)(2,1)}, f32[136,12]{1,0:T(8,128)}) custom-call(bf16[8,136,384]{2,1,0:T(8,128)(2,1)} %reshape_squeeze.3.refs_0_, f32[8,136,12]{2,1,0:T(8,128)} %copy.346.refs_1_), custom_call_target="tpu_custom_call" | custom-call | flops 88780800 | bytes 887808 | tf_op jit(solution)/shard_map/move_7/pallas_call | solution.py:642
  570.4 2.5 reshape.361
  575.4 2.2 reshape.363
  580.1 2.3 add_bitcast_fusion
  594.9 2.3 collective-permute-start.21
  598.3 16.5 %collective-permute-done.17 = bf16[136,1088]{1,0:T(8,128)(2,1)S(1)} collective-permute-done((bf16[136,1088]{1,0:T(8,128)(2,1)S(1)}, bf16[136,1088]{1,0:T(8,128)(2,1)S(1)}, u32[]{:S(2)}, u32[]{:S(2)}) %collective-permute-start.17) | collective-permute-done | bytes 295968 | tf_op jit(solution)/shard_map/ppermute | solution.py:795
  614.8 17.5 %collective-permute-done.18 = bf16[136,1088]{1,0:T(8,128)(2,1)S(1)} collective-permute-done((bf16[136,1088]{1,0:T(8,128)(2,1)S(1)}, bf16[136,1088]{1,0:T(8,128)(2,1)S(1)}, u32[]{:S(2)}, u32[]{:S(2)}) %collective-permute-start.18) | collective-permute-done | bytes 295968 | tf_op jit(solution)/shard_map/ppermute | solution.py:795
  635.1 19.5 %move_8.1 = f32[136,1091]{1,0:T(8,128)} custom-call(bf16[4,136,1091]{2,1,0:T(8,128)(2,1)} %concatenate.73.refs_0_), custom_call_target="tpu_custom_call" | custom-call | flops 118700800 | bytes 1187008 | tf_op jit(solution)/shard_map/move_8/pallas_call | solution.py:642
  660.7 2.5 multiply_subtract_fusion.2
  663.3 2.9 multiply_subtract_fusion.1
  (320 shorter events, 134.7 us)
Async XLA Ops:
  0.7 3.8 copy-start.21
  2.0 3.4 copy-start.22
  3.3 531.7 %copy-start.37 = (f32[128]{0:T(128)}, f32[128]{0:T(128)S(1)}, u32[]{:S(2)}) copy-start(f32[128]{0:T(128)S(1)} %broadcast_multiply_fusion.7) | copy-start | bytes 1540
  4.6 38.4 %copy-start.7 = (f32[1,128,1088]{2,1,0:T(8,128)}, f32[1,128,1088]{2,1,0:T(8,128)S(1)}, u32[]{:S(2)}) copy-start(f32[1,128,1088]{2,1,0:T(8,128)S(1)} %copy.316) | copy-start | bytes 1671172
  6.5 41.9 %copy-start.10 = (f32[136,1088]{1,0:T(8,128)S(1)}, f32[136,1088]{1,0:T(8,128)}, u32[]{:S(2)}) copy-start(f32[136,1088]{1,0:T(8,128)} %param.23) | copy-start | bytes 1775620
  44.2 119.3 %collective-permute-start = (bf16[136,1088]{1,0:T(8,128)(2,1)}, bf16[136,1088]{1,0:T(8,128)(2,1)}, u32[]{:S(2)}, u32[]{:S(2)}) collective-permute-start(bf16[136,1088]{1,0:T(8,128)(2,1)} %reshape.346), channel_id=1, source_target_pairs={{0,2},{1,3},{2,4},{3,5},{4,6},{5,7},{6,0},{7,1},{8,10},{9,11},{10,... | collective-permute-start | bytes 887816 | tf_op jit(solution)/shard_map/ppermute | solution.py:795
  44.2 120.7 %collective-permute-start.1 = (bf16[136,1088]{1,0:T(8,128)(2,1)}, bf16[136,1088]{1,0:T(8,128)(2,1)}, u32[]{:S(2)}, u32[]{:S(2)}) collective-permute-start(bf16[136,1088]{1,0:T(8,128)(2,1)} %reshape.346), channel_id=1, source_target_pairs={{0,4},{1,5},{2,6},{3,7},{4,0},{5,1},{6,2},{7,3},{8,12},{9,13},{10,... | collective-permute-start | bytes 887816 | tf_op jit(solution)/shard_map/ppermute | solution.py:795
  45.8 120.1 %collective-permute-start.2 = (bf16[136,1088]{1,0:T(8,128)(2,1)}, bf16[136,1088]{1,0:T(8,128)(2,1)}, u32[]{:S(2)}, u32[]{:S(2)}) collective-permute-start(bf16[136,1088]{1,0:T(8,128)(2,1)} %reshape.346), channel_id=1, source_target_pairs={{0,6},{1,7},{2,0},{3,1},{4,2},{5,3},{6,4},{7,5},{8,14},{9,15},{10,... | collective-permute-start | bytes 887816 | tf_op jit(solution)/shard_map/ppermute | solution.py:795
  49.3 117.7 %collective-permute-start.11 = (bf16[136,1088]{1,0:T(8,128)(2,1)}, bf16[136,1088]{1,0:T(8,128)(2,1)}, u32[]{:S(2)}, u32[]{:S(2)}) collective-permute-start(bf16[136,1088]{1,0:T(8,128)(2,1)} %get-tuple-element.215), channel_id=1, source_target_pairs={{0,2},{1,3},{2,4},{3,5},{4,6},{5,7},{6,0},{7,1},{8,10},{9,11},{10,... | collective-permute-start | bytes 887816 | tf_op jit(solution)/shard_map/ppermute | solution.py:795
  49.4 119.4 %collective-permute-start.12 = (bf16[136,1088]{1,0:T(8,128)(2,1)}, bf16[136,1088]{1,0:T(8,128)(2,1)}, u32[]{:S(2)}, u32[]{:S(2)}) collective-permute-start(bf16[136,1088]{1,0:T(8,128)(2,1)} %get-tuple-element.215), channel_id=1, source_target_pairs={{0,4},{1,5},{2,6},{3,7},{4,0},{5,1},{6,2},{7,3},{8,12},{9,13},{10,... | collective-permute-start | bytes 887816 | tf_op jit(solution)/shard_map/ppermute | solution.py:795
  130.2 5.4 copy-start.45
  130.2 6.3 copy-start.6
  163.2 12.1 %copy-start.18 = (bf16[128,8,128]{0,2,1:T(8,128)(2,1)}, bf16[128,8,128]{0,2,1:T(8,128)(2,1)S(1)}, u32[]{:S(2)}) copy-start(bf16[128,8,128]{0,2,1:T(8,128)(2,1)S(1)} %copy.328) | copy-start | bytes 786436
  163.5 8.9 %collective-permute-start.13 = (bf16[136,1088]{1,0:T(8,128)(2,1)}, bf16[136,1088]{1,0:T(8,128)(2,1)S(1)}, u32[]{:S(2)}, u32[]{:S(2)}) collective-permute-start(bf16[136,1088]{1,0:T(8,128)(2,1)} %get-tuple-element.215), channel_id=1, source_target_pairs={{0,6},{1,7},{2,0},{3,1},{4,2},{5,3},{6,4},{7,5},{8,14},{9,15},{10,... | collective-permute-start | bytes 887816 | tf_op jit(solution)/shard_map/ppermute | solution.py:795
  167.0 7.4 %collective-permute-start.3 = (bf16[4,136,1088]{2,1,0:T(8,128)(2,1)S(1)}, bf16[4,136,1088]{2,1,0:T(8,128)(2,1)S(1)}, u32[]{:S(2)}, u32[]{:S(2)}) collective-permute-start(bf16[4,136,1088]{2,1,0:T(8,128)(2,1)S(1)} %bitcast_dynamic-update-slice_fusion.13), channel_id=1, source_target_pairs={{0,1},{1,0},{2,3},{3,2},{4,5},{5,4},{6,7},{7,6},{8,9},{9,8},{10,11... | collective-permute-start | bytes 3551240 | tf_op jit(solution)/shard_map/ppermute | solution.py:799
  173.2 22.9 %collective-permute-start.14 = (bf16[4,136,1088]{2,1,0:T(8,128)(2,1)}, bf16[4,136,1088]{2,1,0:T(8,128)(2,1)}, u32[]{:S(2)}, u32[]{:S(2)}) collective-permute-start(bf16[4,136,1088]{2,1,0:T(8,128)(2,1)} %bitcast_dynamic-update-slice_fusion.3), channel_id=1, source_target_pairs={{0,1},{1,0},{2,3},{3,2},{4,5},{5,4},{6,7},{7,6},{8,9},{9,8},{10,11... | collective-permute-start | bytes 3551240 | tf_op jit(solution)/shard_map/ppermute | solution.py:799
  199.2 3.0 copy-start.12
  200.6 3.0 copy-start.47
  228.6 3.4 collective-permute-start.23
  236.2 9.8 %collective-permute-start.24 = (bf16[136,1088]{1,0:T(8,128)(2,1)}, bf16[136,1088]{1,0:T(8,128)(2,1)}, u32[]{:S(2)}, u32[]{:S(2)}) collective-permute-start(bf16[136,1088]{1,0:T(8,128)(2,1)} %get-tuple-element.221), channel_id=1, source_target_pairs={{0,8},{8,16},{16,24},{24,0},{1,9},{9,17},{17,25},{25,1},{2,10},{10... | collective-permute-start | bytes 887816 | tf_op jit(solution)/shard_map/ppermute | solution.py:841
  237.3 16.0 %collective-permute-start.25 = (bf16[136,1088]{1,0:T(8,128)(2,1)}, bf16[136,1088]{1,0:T(8,128)(2,1)S(1)}, u32[]{:S(2)}, u32[]{:S(2)}) collective-permute-start(bf16[136,1088]{1,0:T(8,128)(2,1)} %get-tuple-element.220), channel_id=1, source_target_pairs={{0,16},{8,24},{16,0},{24,8},{1,17},{9,25},{17,1},{25,9},{2,18},{10... | collective-permute-start | bytes 887816 | tf_op jit(solution)/shard_map/ppermute | solution.py:841
  238.5 15.6 %collective-permute-start.26 = (bf16[136,1088]{1,0:T(8,128)(2,1)S(1)}, bf16[136,1088]{1,0:T(8,128)(2,1)S(1)}, u32[]{:S(2)}, u32[]{:S(2)}) collective-permute-start(bf16[136,1088]{1,0:T(8,128)(2,1)S(1)} %get-tuple-element.219), channel_id=1, source_target_pairs={{0,24},{8,0},{16,8},{24,16},{1,25},{9,1},{17,9},{25,17},{2,26},{10... | collective-permute-start | bytes 887816 | tf_op jit(solution)/shard_map/ppermute | solution.py:841
  256.9 8.7 %collective-permute-start.27 = (bf16[136,1088]{1,0:T(8,128)(2,1)}, bf16[136,1088]{1,0:T(8,128)(2,1)S(1)}, u32[]{:S(2)}, u32[]{:S(2)}) collective-permute-start(bf16[136,1088]{1,0:T(8,128)(2,1)} %get-tuple-element.216), channel_id=1, source_target_pairs={{0,2},{1,3},{2,4},{3,5},{4,6},{5,7},{6,0},{7,1},{8,10},{9,11},{10,... | collective-permute-start | bytes 887816 | tf_op jit(solution)/shard_map/ppermute | solution.py:795
  256.9 26.8 %collective-permute-start.28 = (bf16[136,1088]{1,0:T(8,128)(2,1)}, bf16[136,1088]{1,0:T(8,128)(2,1)}, u32[]{:S(2)}, u32[]{:S(2)}) collective-permute-start(bf16[136,1088]{1,0:T(8,128)(2,1)} %get-tuple-element.218), channel_id=1, source_target_pairs={{0,4},{1,5},{2,6},{3,7},{4,0},{5,1},{6,2},{7,3},{8,12},{9,13},{10,... | collective-permute-start | bytes 887816 | tf_op jit(solution)/shard_map/ppermute | solution.py:795
  259.8 28.4 %collective-permute-start.29 = (bf16[136,1088]{1,0:T(8,128)(2,1)}, bf16[136,1088]{1,0:T(8,128)(2,1)}, u32[]{:S(2)}, u32[]{:S(2)}) collective-permute-start(bf16[136,1088]{1,0:T(8,128)(2,1)} %get-tuple-element.217), channel_id=1, source_target_pairs={{0,6},{1,7},{2,0},{3,1},{4,2},{5,3},{6,4},{7,5},{8,14},{9,15},{10,... | collective-permute-start | bytes 887816 | tf_op jit(solution)/shard_map/ppermute | solution.py:795
  293.9 3.6 copy-start.9
  298.7 8.8 %collective-permute-start.4 = (bf16[136,1088]{1,0:T(8,128)(2,1)}, bf16[136,1088]{1,0:T(8,128)(2,1)}, u32[]{:S(2)}, u32[]{:S(2)}) collective-permute-start(bf16[136,1088]{1,0:T(8,128)(2,1)} %reshape.349), channel_id=1, source_target_pairs={{0,2},{1,3},{2,4},{3,5},{4,6},{5,7},{6,0},{7,1},{8,10},{9,11},{10,... | collective-permute-start | bytes 887816 | tf_op jit(solution)/shard_map/ppermute | solution.py:795
  299.7 26.0 %collective-permute-start.5 = (bf16[136,1088]{1,0:T(8,128)(2,1)}, bf16[136,1088]{1,0:T(8,128)(2,1)S(1)}, u32[]{:S(2)}, u32[]{:S(2)}) collective-permute-start(bf16[136,1088]{1,0:T(8,128)(2,1)} %reshape.349), channel_id=1, source_target_pairs={{0,4},{1,5},{2,6},{3,7},{4,0},{5,1},{6,2},{7,3},{8,12},{9,13},{10,... | collective-permute-start | bytes 887816 | tf_op jit(solution)/shard_map/ppermute | solution.py:795
  299.7 26.1 %collective-permute-start.6 = (bf16[136,1088]{1,0:T(8,128)(2,1)}, bf16[136,1088]{1,0:T(8,128)(2,1)S(1)}, u32[]{:S(2)}, u32[]{:S(2)}) collective-permute-start(bf16[136,1088]{1,0:T(8,128)(2,1)} %reshape.349), channel_id=1, source_target_pairs={{0,6},{1,7},{2,0},{3,1},{4,2},{5,3},{6,4},{7,5},{8,14},{9,15},{10,... | collective-permute-start | bytes 887816 | tf_op jit(solution)/shard_map/ppermute | solution.py:795
  327.0 20.1 %copy-start.43 = (f32[136,3]{0,1:T(4,128)S(1)}, f32[136,3]{0,1:T(4,128)}, u32[]{:S(2)}) copy-start(f32[136,3]{0,1:T(4,128)} %param.30) | copy-start | bytes 4900
  327.0 20.9 %copy-start.44 = (f32[136,3]{0,1:T(4,128)S(1)}, f32[136,3]{0,1:T(4,128)}, u32[]{:S(2)}) copy-start(f32[136,3]{0,1:T(4,128)} %param.35) | copy-start | bytes 4900
  328.0 9.2 %collective-permute-start.7 = (bf16[136,1088]{1,0:T(8,128)(2,1)}, bf16[136,1088]{1,0:T(8,128)(2,1)}, u32[]{:S(2)}, u32[]{:S(2)}) collective-permute-start(bf16[136,1088]{1,0:T(8,128)(2,1)} %get-tuple-element.231), channel_id=1, source_target_pairs={{0,8},{8,16},{16,24},{24,0},{1,9},{9,17},{17,25},{25,1},{2,10},{10... | collective-permute-start | bytes 887816 | tf_op jit(solution)/shard_map/ppermute | solution.py:841
  330.1 15.0 %collective-permute-start.8 = (bf16[136,1088]{1,0:T(8,128)(2,1)}, bf16[136,1088]{1,0:T(8,128)(2,1)S(1)}, u32[]{:S(2)}, u32[]{:S(2)}) collective-permute-start(bf16[136,1088]{1,0:T(8,128)(2,1)} %get-tuple-element.230), channel_id=1, source_target_pairs={{0,16},{8,24},{16,0},{24,8},{1,17},{9,25},{17,1},{25,9},{2,18},{10... | collective-permute-start | bytes 887816 | tf_op jit(solution)/shard_map/ppermute | solution.py:841
  331.2 14.6 %collective-permute-start.9 = (bf16[136,1088]{1,0:T(8,128)(2,1)S(1)}, bf16[136,1088]{1,0:T(8,128)(2,1)S(1)}, u32[]{:S(2)}, u32[]{:S(2)}) collective-permute-start(bf16[136,1088]{1,0:T(8,128)(2,1)S(1)} %get-tuple-element.229), channel_id=1, source_target_pairs={{0,24},{8,0},{16,8},{24,16},{1,25},{9,1},{17,9},{25,17},{2,26},{10... | collective-permute-start | bytes 887816 | tf_op jit(solution)/shard_map/ppermute | solution.py:841
  346.6 15.1 %collective-permute-start.10 = (bf16[4,136,1088]{2,1,0:T(8,128)(2,1)}, bf16[4,136,1088]{2,1,0:T(8,128)(2,1)}, u32[]{:S(2)}, u32[]{:S(2)}) collective-permute-start(bf16[4,136,1088]{2,1,0:T(8,128)(2,1)} %bitcast_dynamic-update-slice_fusion.7), channel_id=1, source_target_pairs={{0,1},{1,0},{2,3},{3,2},{4,5},{5,4},{6,7},{7,6},{8,9},{9,8},{10,11... | collective-permute-start | bytes 3551240 | tf_op jit(solution)/shard_map/ppermute | solution.py:799
  366.0 3.6 copy-start.2
  391.7 6.3 copy-start.27
  398.1 3.2 copy-start.13
  427.1 3.3 copy-start.19
  430.4 3.3 copy-start.4
  430.4 4.0 copy-start.49
  456.0 11.6 %copy-start.20 = (bf16[1024,1088]{1,0:T(8,128)(2,1)S(1)}, bf16[1024,1088]{1,0:T(8,128)(2,1)}, u32[]{:S(2)}) copy-start(bf16[1024,1088]{1,0:T(8,128)(2,1)} %fusion.1) | copy-start | bytes 6684676
  476.1 9.8 %copy-start.15 = (bf16[1088,1088]{1,0:T(8,128)(2,1)S(1)}, bf16[1088,1088]{1,0:T(8,128)(2,1)}, u32[]{:S(2)}) copy-start(bf16[1088,1088]{1,0:T(8,128)(2,1)} %convolution_convert_fusion.1) | copy-start | bytes 7102468
  483.1 4.2 copy-start.3
  487.1 105.1 %collective-permute-start.19 = (bf16[4,136,1088]{2,1,0:T(8,128)(2,1)}, bf16[4,136,1088]{2,1,0:T(8,128)(2,1)}, u32[]{:S(2)}, u32[]{:S(2)}) collective-permute-start(bf16[4,136,1088]{2,1,0:T(8,128)(2,1)} %dynamic-slice_bitcast_fusion.1), channel_id=1, source_target_pairs={{0,1},{1,0},{2,3},{3,2},{4,5},{5,4},{6,7},{7,6},{8,9},{9,8},{10,11... | collective-permute-start | bytes 3551240 | tf_op jit(solution)/shard_map/ppermute | solution.py:799
  487.3 4.4 copy-start.25
  488.4 98.2 %collective-permute-start.15 = (bf16[4,136,1088]{2,1,0:T(8,128)(2,1)}, bf16[4,136,1088]{2,1,0:T(8,128)(2,1)}, u32[]{:S(2)}, u32[]{:S(2)}) collective-permute-start(bf16[4,136,1088]{2,1,0:T(8,128)(2,1)} %dynamic-slice_bitcast_fusion.2), channel_id=1, source_target_pairs={{0,1},{1,0},{2,3},{3,2},{4,5},{5,4},{6,7},{7,6},{8,9},{9,8},{10,11... | collective-permute-start | bytes 3551240 | tf_op jit(solution)/shard_map/ppermute | solution.py:799
  500.8 34.3 %copy-start.41 = (f32[128]{0:T(128)S(1)}, f32[128]{0:T(128)}, u32[]{:S(2)}) copy-start(f32[128]{0:T(128)} %copy-done.40) | copy-start | bytes 1540
  500.8 36.7 %copy-start.39 = (f32[1088]{0:T(1024)S(1)}, f32[1088]{0:T(1024)}, u32[]{:S(2)}) copy-start(f32[1088]{0:T(1024)} %get-tuple-element.243) | copy-start | bytes 13060
  575.4 3.6 copy-start.34
  575.4 4.6 copy-start.1
  575.4 4.6 copy-start.5
  586.6 5.7 copy-start.16
  588.8 8.3 %collective-permute-start.16 = (bf16[136,1088]{1,0:T(8,128)(2,1)S(1)}, bf16[136,1088]{1,0:T(8,128)(2,1)S(1)}, u32[]{:S(2)}, u32[]{:S(2)}) collective-permute-start(bf16[136,1088]{1,0:T(8,128)(2,1)S(1)} %get-tuple-element.226), channel_id=1, source_target_pairs={{0,2},{1,3},{2,4},{3,5},{4,6},{5,7},{6,0},{7,1},{8,10},{9,11},{10,... | collective-permute-start | bytes 887816 | tf_op jit(solution)/shard_map/ppermute | solution.py:795
  588.9 25.9 %collective-permute-start.17 = (bf16[136,1088]{1,0:T(8,128)(2,1)S(1)}, bf16[136,1088]{1,0:T(8,128)(2,1)S(1)}, u32[]{:S(2)}, u32[]{:S(2)}) collective-permute-start(bf16[136,1088]{1,0:T(8,128)(2,1)S(1)} %get-tuple-element.228), channel_id=1, source_target_pairs={{0,4},{1,5},{2,6},{3,7},{4,0},{5,1},{6,2},{7,3},{8,12},{9,13},{10,... | collective-permute-start | bytes 887816 | tf_op jit(solution)/shard_map/ppermute | solution.py:795
  590.8 41.4 %collective-permute-start.18 = (bf16[136,1088]{1,0:T(8,128)(2,1)S(1)}, bf16[136,1088]{1,0:T(8,128)(2,1)S(1)}, u32[]{:S(2)}, u32[]{:S(2)}) collective-permute-start(bf16[136,1088]{1,0:T(8,128)(2,1)S(1)} %get-tuple-element.227), channel_id=1, source_target_pairs={{0,6},{1,7},{2,0},{3,1},{4,2},{5,3},{6,4},{7,5},{8,14},{9,15},{10,... | collective-permute-start | bytes 887816 | tf_op jit(solution)/shard_map/ppermute | solution.py:795
  594.8 68.4 %collective-permute-start.20 = (bf16[136,1088]{1,0:T(8,128)(2,1)}, bf16[136,1088]{1,0:T(8,128)(2,1)}, u32[]{:S(2)}, u32[]{:S(2)}) collective-permute-start(bf16[136,1088]{1,0:T(8,128)(2,1)} %get-tuple-element.223), channel_id=1, source_target_pairs={{0,2},{1,3},{2,4},{3,5},{4,6},{5,7},{6,0},{7,1},{8,10},{9,11},{10,... | collective-permute-start | bytes 887816 | tf_op jit(solution)/shard_map/ppermute | solution.py:795
  594.9 68.3 %collective-permute-start.21 = (bf16[136,1088]{1,0:T(8,128)(2,1)}, bf16[136,1088]{1,0:T(8,128)(2,1)}, u32[]{:S(2)}, u32[]{:S(2)}) collective-permute-start(bf16[136,1088]{1,0:T(8,128)(2,1)} %get-tuple-element.225), channel_id=1, source_target_pairs={{0,4},{1,5},{2,6},{3,7},{4,0},{5,1},{6,2},{7,3},{8,12},{9,13},{10,... | collective-permute-start | bytes 887816 | tf_op jit(solution)/shard_map/ppermute | solution.py:795
  597.1 66.1 %collective-permute-start.22 = (bf16[136,1088]{1,0:T(8,128)(2,1)}, bf16[136,1088]{1,0:T(8,128)(2,1)}, u32[]{:S(2)}, u32[]{:S(2)}) collective-permute-start(bf16[136,1088]{1,0:T(8,128)(2,1)} %get-tuple-element.224), channel_id=1, source_target_pairs={{0,6},{1,7},{2,0},{3,1},{4,2},{5,3},{6,4},{7,5},{8,14},{9,15},{10,... | collective-permute-start | bytes 887816 | tf_op jit(solution)/shard_map/ppermute | solution.py:795
  632.9 21.7 %copy-start.33 = (f32[136,3]{1,0:T(8,128)S(1)}, f32[136,3]{1,0:T(8,128)}, u32[]{:S(2)}) copy-start(f32[136,3]{1,0:T(8,128)} %copy.363) | copy-start | bytes 4900
  632.9 25.5 %copy-start.29 = (f32[136,272]{1,0:T(8,128)S(1)}, f32[136,272]{1,0:T(8,128)}, u32[]{:S(2)}) copy-start(f32[136,272]{1,0:T(8,128)} %param.22) | copy-start | bytes 443908
  635.1 25.6 %copy-start.23 = (f32[136,816]{1,0:T(8,128)S(1)}, f32[136,816]{1,0:T(8,128)}, u32[]{:S(2)}) copy-start(f32[136,816]{1,0:T(8,128)} %param.21) | copy-start | bytes 1331716
  635.1 25.6 %copy-start.32 = (f32[136,816]{1,0:T(8,128)S(1)}, f32[136,816]{1,0:T(8,128)}, u32[]{:S(2)}) copy-start(f32[136,816]{1,0:T(8,128)} %param.26) | copy-start | bytes 1331716
  654.6 6.0 copy-start.8
  (16 other events, 33.1 us)

commit v2 on v1

--- a/solution.py
+++ b/solution.py
@@ -370,7 +370,7 @@
     chip = lax.div(me_c, 2)
     core = lax.rem(me_c, 2)
     found = []
-    if any(kind.endswith("dp") for kind in kinds):
+    if any("dp" in kind for kind in kinds):
         found += [{"dp": lax.rem(me_d + r, m)} for r in range(1, m)]
     if "swap_ctx" in kinds:
         found += [{"ctx": lax.rem(me_c + r, n)} for r in range(1, n)]
@@ -425,7 +425,7 @@
     def keep(self):
         self.out[self.me] = self.x[...]
 
-    def middle(self):
+    def middle(self, t):
         pass
 
     def finish(self):
@@ -481,16 +481,45 @@
         )
 
 
-class GatherCtx:
-    scratch = 0
-
-    def __init__(self, x, out, sems):
-        self.x, self.out, self.sems = x, out, sems
+class Line:
+    def setup(self):
         self.chips = lax.axis_size("ctx") // 2
         self.me = lax.axis_index("ctx")
         self.chip = lax.div(self.me, 2)
         self.core = lax.rem(self.me, 2)
         self.partner = 2 * self.chip + 1 - self.core
+        self.sent = []
+
+    def launch(self, copy, when=None):
+        self.sent.append((copy, when))
+        if when is None:
+            copy.start()
+        else:
+            pl.when(when)(copy.start)
+
+    def drain(self):
+        for copy, when in self.sent:
+            if when is None:
+                copy.wait_send()
+            else:
+                pl.when(when)(copy.wait_send)
+
+    def sides(self):
+        return (
+            (1, self.chip < self.chips - 1, self.chip > 0),
+            (-1, self.chip > 0, self.chip < self.chips - 1),
+        )
+
+    def safe(self, chip):
+        return lax.min(lax.max(chip, 0), self.chips - 1)
+
+
+class GatherCtx(Line):
+    scratch = 0
+
+    def __init__(self, x, out, sems):
+        self.x, self.out, self.sems = x, out, sems
+        self.setup()
 
     def of_chip(self, r, core):
         return 2 * lax.rem(self.chip + self.chips + r, self.chips) + core
@@ -501,38 +530,105 @@
         )
 
     def start(self):
-        self.sent = []
-        for r in range(1, self.chips):
-            copy = self.copy(self.x, r, self.me, self.of_chip(r, self.core))
-            copy.start()
-            self.sent.append(copy)
-        copy = self.copy(self.x, 0, self.me, self.partner)
-        copy.start()
-        self.sent.append(copy)
+        for side, onward, _ in self.sides():
+            to = 2 * self.safe(self.chip + side) + self.core
+            self.launch(self.copy(self.x, (side + 1) // 2, self.me, to), onward)
+        self.launch(self.copy(self.x, 2, self.me, self.partner))
         self.out[self.me] = self.x[...]
 
-    def middle(self):
-        for r in range(1, self.chips):
-            of = self.of_chip(-r, self.core)
-            self.copy(self.x, r, of, of).wait_recv()
-            copy = self.copy(self.out.at[of], self.chips + r, of, self.partner)
-            copy.start()
-            self.sent.append(copy)
+    def middle(self, t):
+        for side, onward, _ in self.sides():
+            chip = self.chip - side * t
+            here = (chip >= 0) & (chip < self.chips)
+            of = 2 * self.safe(chip) + self.core
+            slot = 3 + 4 * (t - 1) + (side + 1)
+            pl.when(here)(self.copy(self.x, slot, of, of).wait_recv)
+            to = 2 * self.safe(self.chip + side) + self.core
+            self.launch(self.copy(self.out.at[of], slot, of, to), here & onward)
+            self.launch(self.copy(self.out.at[of], slot + 1, of, self.partner), here)
 
     def finish(self):
         for r in range(self.chips):
             of = self.of_chip(-r, 1 - self.core)
-            self.copy(self.x, 0, of, self.partner).wait_recv()
-        for copy in self.sent:
-            copy.wait_send()
-
-
-class SumCtx(GatherCtx):
+            self.copy(self.x, 2, of, self.partner).wait_recv()
+        self.drain()
+
+
+class ShrinkGather(Line):
+    scratch = 1
+
+    def __init__(self, x, out, sems, line):
+        self.x, self.out, self.sems, self.line = x, out, sems, line
+        self.setup()
+        self.m = lax.axis_size("dp")
+        self.row = lax.axis_index("dp")
+
+    def along(self, src, slot, of, to):
+        return send(
+            src, self.line.at[of], self.sems[0].at[slot], self.sems[1].at[of],
+            {"ctx": 2 * to + self.core},
+        )
+
+    def across(self, src, slot, of, to):
+        return send(
+            src, self.out.at[of, self.core], self.sems[0].at[slot],
+            self.sems[1].at[self.chips + of], {"dp": to},
+        )
+
+    def over(self, slot, of, core):
+        return send(
+            self.out.at[of, core], self.out.at[of, core], self.sems[0].at[slot],
+            self.sems[1].at[self.chips + self.m + of], {"ctx": self.partner},
+        )
+
+    def place(self, src, chip, slot, when):
+        mine = chip == self.row
+        ok = mine if when is None else when & mine
+
+        @pl.when(ok)
+        def _():
+            self.out[self.row, self.core] = src[...]
+
+        other = chip != self.row
+        to = lax.rem(chip + 0 * self.row, self.m)
+        self.launch(self.across(src, slot, self.row, to), other if when is None else when & other)
+
+    def start(self):
+        for side, onward, _ in self.sides():
+            to = self.safe(self.chip + side)
+            self.launch(self.along(self.x, (side + 1) // 2, self.chip, to), onward)
+        self.place(self.x, self.chip, 2, None)
+
+    def middle(self, t):
+        for side, onward, _ in self.sides():
+            chip = self.chip - side * t
+            here = (chip >= 0) & (chip < self.chips)
+            of = self.safe(chip)
+            slot = 3 + 4 * (t - 1) + (side + 1)
+            pl.when(here)(self.along(self.x, slot, of, of).wait_recv)
+            to = self.safe(self.chip + side)
+            self.launch(self.along(self.line.at[of], slot, of, to), here & onward)
+            self.place(self.line.at[of], of, slot + 1, here)
+
+    def finish(self):
+        base = 3 + 4 * (self.chips - 1)
+        self.launch(self.over(base, self.row, self.core))
+        for r in range(1, self.m):
+            of = lax.rem(self.row + r, self.m)
+            self.across(self.x, 2, of, of).wait_recv()
+            self.launch(self.over(base + r, of, self.core))
+        for of in range(self.m):
+            self.over(base, of, 1 - self.core).wait_recv()
+        self.drain()
+
+
+class SumCtx(Line):
     scratch = 3
 
     def __init__(self, x, out, sems, half, pre, got):
-        super().__init__(x, out, sems)
+        self.x, self.out, self.sems = x, out, sems
         self.half, self.pre, self.got = half, pre, got
+        self.setup()
 
     def early(self, r):
         j = lax.rem(self.chip + r, self.chips)
@@ -554,23 +650,15 @@
         )
 
     def start(self):
-        self.sent = []
         for r in list(range(1, self.chips)) + [0]:
-            copy = self.early(r)
-            copy.start()
-            self.sent.append(copy)
-
-    def middle(self):
-        for r in range(1, self.chips):
-            self.early(r).wait_recv()
-            to = lax.rem(self.chip + r, self.chips)
-            total = self.x[2 * to + self.core].astype(jnp.float32) + self.half[to].astype(
-                jnp.float32
-            )
-            self.pre[to] = total.astype(self.pre.dtype)
-            copy = self.late(r, self.chip, to)
-            copy.start()
-            self.sent.append(copy)
+            self.launch(self.early(r))
+
+    def middle(self, r):
+        self.early(r).wait_recv()
+        to = lax.rem(self.chip + r, self.chips)
+        total = self.x[2 * to + self.core].astype(jnp.float32) + self.half[to].astype(jnp.float32)
+        self.pre[to] = total.astype(self.pre.dtype)
+        self.launch(self.late(r, self.chip, to))
 
     def finish(self):
         self.early(0).wait_recv()
@@ -580,8 +668,135 @@
             self.late(r, of, of).wait_recv()
             total = total + self.got[of].astype(jnp.float32)
         self.out[...] = total
-        for copy in self.sent:
-            copy.wait_send()
+        self.drain()
+
+
+class ShrinkCross(Line):
+    scratch = 2
+
+    def __init__(self, x, out, sems, half, pre):
+        self.x, self.out, self.sems = x, out, sems
+        self.half, self.pre = half, pre
+        self.setup()
+        self.m = lax.axis_size("dp")
+        self.row = lax.axis_index("dp")
+
+    def early(self, r):
+        j = lax.rem(self.row + r, self.m)
+        return send(
+            self.x.at[j, 1 - self.core],
+            self.half.at[j],
+            self.sems[0].at[r],
+            self.sems[1].at[j],
+            {"ctx": self.partner},
+        )
+
+    def across(self, r, of, to):
+        return send(
+            self.pre.at[to],
+            self.out.at[of],
+            self.sems[0].at[self.m + r],
+            self.sems[1].at[self.m + of],
+            {"dp": to},
+        )
+
+    def add(self, j):
+        total = self.x[j, self.core].astype(jnp.float32) + self.half[j].astype(jnp.float32)
+        return total.astype(self.pre.dtype)
+
+    def start(self):
+        for r in list(range(1, self.m)) + [0]:
+            self.launch(self.early(r))
+
+    def middle(self, r):
+        self.early(r).wait_recv()
+        to = lax.rem(self.row + r, self.m)
+        self.pre[to] = self.add(to)
+        self.launch(self.across(r, self.row, to))
+
+    def finish(self):
+        self.early(0).wait_recv()
+        self.out[self.row] = self.add(self.row)
+        for r in range(1, self.m):
+            of = lax.rem(self.row + self.m - r, self.m)
+            self.across(r, of, of).wait_recv()
+        self.drain()
+
+
+class LineSum(Line):
+    scratch = 1
+
+    def __init__(self, x, out, sems, got):
+        self.x, self.out, self.sems, self.got = x, out, sems, got
+        self.setup()
+
+    def along(self, r, of, to):
+        return send(
+            self.x.at[to],
+            self.got.at[of],
+            self.sems[0].at[r],
+            self.sems[1].at[of],
+            {"ctx": 2 * to + self.core},
+        )
+
+    def start(self):
+        for r in range(1, self.chips):
+            self.launch(self.along(r, self.chip, lax.rem(self.chip + r, self.chips)))
+
+    def middle(self, t):
+        pass
+
+    def finish(self):
+        total = self.x[self.chip].astype(jnp.float32)
+        for r in range(1, self.chips):
+            of = lax.rem(self.chip + self.chips - r, self.chips)
+            self.along(r, of, of).wait_recv()
+            total = total + self.got[of].astype(jnp.float32)
+        self.out[...] = total
+        self.drain()
+
+
+class HalfGather(Line):
+    scratch = 0
+
+    def __init__(self, x, out, sems):
+        self.x, self.out, self.sems = x, out, sems
+        self.setup()
+        self.m = lax.axis_size("dp")
+        self.row = lax.axis_index("dp")
+
+    def across(self, r, of, to):
+        return send(
+            self.x.at[self.core],
+            self.out.at[of, self.core],
+            self.sems[0].at[r],
+            self.sems[1].at[of],
+            {"dp": to},
+        )
+
+    def over(self, r, of, core):
+        return send(
+            self.out.at[of, core],
+            self.out.at[of, core],
+            self.sems[0].at[self.m + r],
+            self.sems[1].at[self.m + of],
+            {"ctx": self.partner},
+        )
+
+    def start(self):
+        for r in range(1, self.m):
+            self.launch(self.across(r, self.row, lax.rem(self.row + r, self.m)))
+        self.out[self.row] = self.x[...]
+
+    def middle(self, r):
+        of = lax.rem(self.row + self.m - r, self.m)
+        self.across(r, of, of).wait_recv()
+        self.launch(self.over(r, of, self.core))
+
+    def finish(self):
+        for r in range(1, self.m):
+            self.over(r, lax.rem(self.row + r, self.m), 1 - self.core).wait_recv()
+        self.drain()
 
 
 MOVES = {
@@ -591,6 +806,10 @@
     "gather_ctx": GatherCtx,
     "swap_ctx": SwapCtx,
     "sum_ctx": SumCtx,
+    "shrink_gather_dp_ctx": ShrinkGather,
+    "shrink_cross_dp_ctx": ShrinkCross,
+    "line_sum_ctx": LineSum,
+    "half_gather_dp_ctx": HalfGather,
 }
 
 
@@ -611,8 +830,9 @@
         moves.append(MOVES[kind](x, out, sems, *extra))
     for move in moves:
         move.start()
-    for move in moves:
-        move.middle()
+    for t in range(1, lax.axis_size("ctx") // 2):
+        for move in moves:
+            move.middle(t)
     for move in moves:
         move.finish()
 
@@ -624,20 +844,37 @@
     shapes, scratch, sent = [], [], 0
     for kind, x in pairs:
         size = n if kind.endswith("ctx") else m
-        if kind.startswith("gather"):
-            shapes.append(jax.ShapeDtypeStruct((size,) + x.shape, x.dtype))
-            sent += (size - 1) * x.size * x.dtype.itemsize
+        one = x.dtype
+        semaphores = size
+        sent += x.size * x.dtype.itemsize
+        extra = []
+        if kind == "shrink_gather_dp_ctx":
+            shape = jax.ShapeDtypeStruct((m, 2) + x.shape, one)
+            extra = [pltpu.VMEM((n // 2,) + x.shape, one)]
+            semaphores = 2 * n + m
+        elif kind == "shrink_cross_dp_ctx":
+            shape = jax.ShapeDtypeStruct((m,) + x.shape[2:], one)
+            extra = [pltpu.VMEM((m,) + x.shape[2:], one)] * 2
+            semaphores = 2 * m
+        elif kind == "line_sum_ctx":
+            shape = jax.ShapeDtypeStruct(x.shape[1:], jnp.float32)
+            extra = [pltpu.VMEM(x.shape, one)]
+        elif kind == "half_gather_dp_ctx":
+            shape = jax.ShapeDtypeStruct((m,) + x.shape, one)
+            semaphores = 2 * m
+        elif kind.startswith("gather"):
+            shape = jax.ShapeDtypeStruct((size,) + x.shape, one)
+            semaphores = 2 * size
         elif kind.startswith("swap"):
-            shapes.append(jax.ShapeDtypeStruct(x.shape, x.dtype))
-            sent += x.size * x.dtype.itemsize
+            shape = jax.ShapeDtypeStruct(x.shape, one)
         else:
-            shapes.append(jax.ShapeDtypeStruct(x.shape[1:], jnp.float32))
-            sent += x.size * x.dtype.itemsize
-        scratch += [pltpu.SemaphoreType.DMA((size,)), pltpu.SemaphoreType.DMA((size,))]
-        if kind == "sum_dp":
-            scratch += [pltpu.VMEM(x.shape, x.dtype)]
-        if kind == "sum_ctx":
-            scratch += [pltpu.VMEM((n // 2,) + x.shape[1:], x.dtype)] * 3
+            shape = jax.ShapeDtypeStruct(x.shape[1:], jnp.float32)
+            if kind == "sum_dp":
+                extra = [pltpu.VMEM(x.shape, one)]
+            else:
+                extra = [pltpu.VMEM((n // 2,) + x.shape[1:], one)] * 3
+        shapes.append(shape)
+        scratch += [pltpu.SemaphoreType.DMA((semaphores,))] * 2 + extra
     kernel = lambda *refs: move_kernel(kinds, *refs)
     return pl.pallas_call(
         kernel,
@@ -663,31 +900,32 @@
     return row >= lax.broadcasted_iota(jnp.int32, shape, 1)
 
 
-def sort_rows(order_ref, src, dst):
+def sort_rows(order_ref, src, dst, lane):
     for b in range(src.shape[0] // BLK):
         start = pl.multiple_of(order_ref[b] * BLK, BLK)
-        dst[b * BLK : (b + 1) * BLK, :] = src[pl.ds(start, BLK), :]
-
-
-def unsort_rows(order_ref, src, dst):
+        dst[b * BLK : (b + 1) * BLK, lane : lane + src.shape[1]] = src[pl.ds(start, BLK), :]
+
+
+def unsort_rows(order_ref, src, dst, lane):
     for b in range(dst.shape[0] // BLK):
         start = pl.multiple_of(order_ref[b] * BLK, BLK)
-        dst[pl.ds(start, BLK), :] = src[b * BLK : (b + 1) * BLK, :]
+        dst[pl.ds(start, BLK), :] = src[b * BLK : (b + 1) * BLK, lane : lane + dst.shape[1]]
 
 
 def head_slots():
     return ((0, 0), (0, 1), (1, 0))
 
 
-def pairs_forward(order_ref, qkv_ref, out_ref, log_ref, rows, outs):
-    sort_rows(order_ref, qkv_ref, rows)
-    seq = qkv_ref.shape[0]
+def pairs_forward(order_ref, main_ref, last_ref, out_ref, log_ref, rows, outs):
+    sort_rows(order_ref, main_ref, rows, 0)
+    sort_rows(order_ref, last_ref, rows, 3 * TILE)
+    seq = main_ref.shape[0]
     step = min(4 * BLK, seq)
     for i in range(seq // step):
         at = slice(i * step, (i + 1) * step)
         results, logs = [], []
         for block, half in head_slots():
-            lanes = lambda part: slice((2 * part + block) * TILE, (2 * part + block + 1) * TILE)
+            lanes = lambda part: slice((3 * block + part) * TILE, (3 * block + part + 1) * TILE)
             query = rows[at, lanes(0)] * HD ** (-0.5)
             query = query.astype(jnp.bfloat16)
             if block == 0:
@@ -716,16 +954,30 @@
         outs[at, TILE:] = results[2].astype(jnp.bfloat16)
         lane = lax.broadcasted_iota(jnp.int32, (step, TILE), 1)
         log_ref[at, :] = jnp.where(lane == 0, logs[0], jnp.where(lane == 1, logs[1], logs[2]))
-    unsort_rows(order_ref, outs, out_ref)
+    unsort_rows(order_ref, outs, out_ref, 0)
 
 
 def pairs_backward(
-    order_ref, qkv_ref, out_ref, log_ref, dout_ref, dqkv_ref, rows, outs, douts, grads, dkey, dvalue
+    order_ref,
+    main_ref,
+    last_ref,
+    out_ref,
+    log_ref,
+    dout_ref,
+    dmain_ref,
+    dlast_ref,
+    rows,
+    outs,
+    douts,
+    grads,
+    dkey,
+    dvalue,
 ):
-    sort_rows(order_ref, qkv_ref, rows)
-    sort_rows(order_ref, out_ref, outs)
-    sort_rows(order_ref, dout_ref, douts)
-    seq = qkv_ref.shape[0]
+    sort_rows(order_ref, main_ref, rows, 0)
+    sort_rows(order_ref, last_ref, rows, 3 * TILE)
+    sort_rows(order_ref, out_ref, outs, 0)
+    sort_rows(order_ref, dout_ref, douts, 0)
+    seq = main_ref.shape[0]
     step = min(4 * BLK, seq)
     dkey[...] = jnp.zeros_like(dkey)
     dvalue[...] = jnp.zeros_like(dvalue)
@@ -733,7 +985,7 @@
         at = slice(i * step, (i + 1) * step)
         dqueries = []
         for slot, (block, half) in enumerate(head_slots()):
-            lanes = lambda part: slice((2 * part + block) * TILE, (2 * part + block + 1) * TILE)
+            lanes = lambda part: slice((3 * block + part) * TILE, (3 * block + part + 1) * TILE)
             own = slice(block * TILE, (block + 1) * TILE)
             query = (rows[at, lanes(0)] * HD ** (-0.5)).astype(jnp.bfloat16)
             dout = douts[at, own]
@@ -763,12 +1015,13 @@
         first = pair_lanes((step, TILE), 0)
         grads[at, :TILE] = jnp.where(first, dqueries[0], dqueries[1]).astype(jnp.bfloat16)
         third = jnp.where(first, dqueries[2], 0.0)
-        grads[at, TILE : 2 * TILE] = third.astype(jnp.bfloat16)
+        grads[at, 3 * TILE : 4 * TILE] = third.astype(jnp.bfloat16)
     for block in range(2):
         own = slice(block * TILE, (block + 1) * TILE)
-        grads[:, (2 + block) * TILE : (3 + block) * TILE] = dkey[own, :].T.astype(jnp.bfloat16)
-        grads[:, (4 + block) * TILE : (5 + block) * TILE] = dvalue[own, :].T.astype(jnp.bfloat16)
-    unsort_rows(order_ref, grads, dqkv_ref)
+        grads[:, (3 * block + 1) * TILE : (3 * block + 2) * TILE] = dkey[own, :].T.astype(jnp.bfloat16)
+        grads[:, (3 * block + 2) * TILE : (3 * block + 3) * TILE] = dvalue[own, :].T.astype(jnp.bfloat16)
+    unsort_rows(order_ref, grads, dmain_ref, 0)
+    unsort_rows(order_ref, grads, dlast_ref, 3 * TILE)
 
 
 def attend(kernel, order, arrays, shapes, scratch, matmuls):
@@ -788,59 +1041,15 @@
     )(order, *arrays)
 
 
-def turn(x, r):
-    n = lax.axis_size("ctx")
-    chips = n // 2
-    pairs = [(2 * q + k, 2 * ((q + r) % chips) + k) for q in range(chips) for k in range(2)]
-    return lax.ppermute(x, "ctx", pairs)
-
-
 def trade(x):
     return lax.ppermute(x, "ctx", [(c, c ^ 1) for c in range(lax.axis_size("ctx"))])
 
 
-def line_gather(x):
-    chips = lax.axis_size("ctx") // 2
-    chip = lax.axis_index("ctx") // 2
-    out = jnp.zeros((chips,) + x.shape, x.dtype)
-    for r in range(chips):
-        piece = x if r == 0 else turn(x, r)
-        out = lax.dynamic_update_index_in_dim(out, piece, (chip - r) % chips, 0)
-    return out
-
-
-def line_sum(x):
-    chips = lax.axis_size("ctx") // 2
-    chip = lax.axis_index("ctx") // 2
-    total = lax.dynamic_index_in_dim(x, chip, 0, False).astype(jnp.float32)
-    for r in range(1, chips):
-        piece = lax.dynamic_index_in_dim(x, (chip + r) % chips, 0, False)
-        total = total + turn(piece, r).astype(jnp.float32)
-    return total
-
-
-def both_cores(x, other, axis):
-    core = lax.axis_index("ctx") % 2
-    return jnp.where(core == 0, jnp.stack([x, other], axis), jnp.stack([other, x], axis))
-
-
-def core_sum(x, axis):
-    core = lax.axis_index("ctx") % 2
-    mine = lax.dynamic_index_in_dim(x, core, axis, False)
-    other = lax.dynamic_index_in_dim(x, 1 - core, axis, False)
-    return (mine.astype(jnp.float32) + trade(other).astype(jnp.float32)).astype(x.dtype)
-
-
-def swap_dp(x):
-    m = lax.axis_size("dp")
-    me = lax.axis_index("dp")
-    out = jnp.zeros_like(x)
-    for r in range(m):
-        piece = lax.dynamic_index_in_dim(x, (me + r) % m, 0, False)
-        if r:
-            piece = lax.ppermute(piece, "dp", [(d, (d + r) % m) for d in range(m)])
-        out = lax.dynamic_update_index_in_dim(out, piece, (me - r) % m, 0)
-    return out
+def core_pair(mine, other, axis):
+    first = lax.axis_index("ctx") % 2 == 0
+    return jnp.where(
+        first, jnp.concatenate([mine, other], axis), jnp.concatenate([other, mine], axis)
+    )
 
 
 def local_pairs(
@@ -869,7 +1078,6 @@
     m = lax.axis_size("dp")
     here = lax.axis_index("ctx")
     seq_here = lax.axis_index("dp")
-    chips = n // 2
     rows = inputs.shape[1]
     total = rows * n
     feat = D // n
@@ -888,51 +1096,53 @@
     order = jnp.sum(jnp.where(flat[None, :] == blocks[:, None], blocks[None, :], 0), axis=1)
 
     w_expand_own = expand_weight.astype(bf16)
-    w_shrink_own = (
-        shrink_weight.astype(bf16)
-        .T.reshape(fold, cols // fold, hid)
-        .transpose(1, 0, 2)
-        .reshape(cols // fold, wide)
+    first_core = here % 2 == 0
+    shrink_t = shrink_weight.astype(bf16).T
+    upper, lower = shrink_t[: cols // fold], shrink_t[cols // fold :]
+    w_shrink_own = core_pair(
+        jnp.where(first_core, upper, lower), trade(jnp.where(first_core, lower, upper)), 1
     )
     packed = jnp.concatenate(
-        [triple_weight.astype(bf16), merge_weight.astype(bf16), vector_params.astype(bf16)], axis=1
+        [triple_weight.astype(bf16), vector_params.astype(bf16)], axis=1
     )
     normed_one, inverse_one = layer_norm(stream)
     cot_b = cotangent.astype(bf16)
-    normed_full, columns, cot_full = move(
-        0, ("gather_ctx", normed_one.astype(bf16)), ("gather_dp", packed), ("gather_dp", cot_b)
+    normed_full, w_expand, merge_line, columns, cot_full = move(
+        0,
+        ("gather_ctx", normed_one.astype(bf16)),
+        ("gather_ctx", w_expand_own),
+        ("gather_ctx", merge_weight.astype(bf16)),
+        ("gather_dp", packed),
+        ("gather_dp", cot_b),
     )
     normed_full = normed_full.reshape(total, D)
     cot_full = cot_full.reshape(m * rows, D)
-
-    expand_line = line_gather(w_expand_own)
-    w_expand = both_cores(expand_line, trade(expand_line), 1).reshape(D, wide)
-    shrink_line = swap_dp(line_gather(w_shrink_own))
-    w_shrink_t = (
-        both_cores(shrink_line, trade(shrink_line), 1)
-        .reshape(m, fold, cols // fold, fold, hid)
-        .transpose(0, 3, 2, 1, 4)
-        .reshape(D, wide)
-    )
+    w_expand = w_expand.reshape(D, wide)
 
     def take(start, width):
         return columns[:, :, start : start + width].transpose(1, 0, 2).reshape(feat, m * width)
 
     triple_rows = take(0, tw).reshape(feat, 3, D)
-    merge_rows = take(tw, mw)
-    vector_rows = take(tw + mw, vector_params.shape[1])
+    vector_rows = take(tw, vector_params.shape[1])
     slabs = (
         triple_rows[:, :, :cut].reshape(feat, 3, n, TILE).transpose(2, 0, 1, 3).reshape(n, feat, -1)
     )
     common = jnp.concatenate([triple_rows[:, :, cut:].reshape(feat, 3 * spare), vector_rows], axis=1)
-    w_main, w_common = move(1, ("swap_ctx", slabs), ("gather_ctx", common))
-    merge_line = line_gather(merge_rows)
-    w_merge = both_cores(merge_line, trade(merge_line), 1).reshape(D, D)
-    w_main = w_main.reshape(D, 3, TILE)
+    w_main, w_common, w_merge, w_shrink_t = move(
+        1,
+        ("swap_ctx", slabs),
+        ("gather_ctx", common),
+        ("half_gather_dp_ctx", merge_line.reshape(2, D // 2, mw)),
+        ("shrink_gather_dp_ctx", w_shrink_own),
+    )
+    w_shrink_t = w_shrink_t.reshape(D, wide)
+    w_merge = w_merge.reshape(m, D, mw).transpose(1, 0, 2).reshape(D, D)
+    w_main = w_main.reshape(D, 3 * TILE)
     w_common = w_common.reshape(D, -1)
-    w_last = w_common[:, : 3 * spare].reshape(D, 3, spare)
-    w_last = jnp.pad(w_last, ((0, 0), (0, 0), (0, TILE - spare)))
-    w_triple = jnp.concatenate([w_main, w_last], axis=2).reshape(D, 6 * TILE)
+    near = lax.broadcasted_iota(jnp.int32, (w_common.shape[1], 3 * TILE), 0)
+    far = lax.broadcasted_iota(jnp.int32, (w_common.shape[1], 3 * TILE), 1)
+    spread = (far % TILE < spare) & (near == far // TILE * spare + far % TILE)
+    w_last = dot_on(w_common, spread.astype(bf16), 1, 0).astype(bf16)
     vectors = w_common[:, 3 * spare :].astype(f32)
     gain_one = vectors[:, 0]
     shift_one = vectors[:, 1]
@@ -942,21 +1152,24 @@
     shrink_bias = vectors[:, 7]
     expand_bias = lax.dynamic_slice_in_dim(vectors[:, 8:].T.reshape(-1), seq_here * wide, wide)
 
-    def own_bias(column):
-        main = lax.dynamic_slice_in_dim(vectors[:, column], here * TILE, TILE)
-        last = jnp.pad(vectors[cut:, column], (0, TILE - spare))
-        return jnp.concatenate([main, last])
-
-    zeros = jnp.zeros((2 * TILE,), f32)
-    bias = jnp.concatenate([own_bias(2), zeros, own_bias(3)])
+    def main_bias(column):
+        return lax.dynamic_slice_in_dim(vectors[:, column], here * TILE, TILE)
+
+    def last_bias(column):
+        return jnp.pad(vectors[cut:, column], (0, TILE - spare))
+
+    zeros = jnp.zeros((TILE,), f32)
+    bias_main = jnp.concatenate([main_bias(2), zeros, main_bias(3)])
+    bias_last = jnp.concatenate([last_bias(2), zeros, last_bias(3)])
     act_one = (normed_full.astype(f32) * gain_one + shift_one).astype(bf16)
-    qkv = (dot_on(act_one, w_triple, 1, 0) + bias).astype(bf16)
+    qkv_main = (dot_on(act_one, w_main, 1, 0) + bias_main).astype(bf16)
+    qkv_last = (dot_on(act_one, w_last, 1, 0) + bias_last).astype(bf16)
     rows_scratch = pltpu.VMEM((total, 6 * TILE), bf16)
     half_scratch = pltpu.VMEM((total, 2 * TILE), bf16)
     attended, log_total = attend(
         pairs_forward,
         order,
-        (qkv,),
+        (qkv_main, qkv_last),
         [
             jax.ShapeDtypeStruct((total, 2 * TILE), bf16),
             jax.ShapeDtypeStruct((total, TILE), f32),
@@ -979,21 +1192,12 @@
     dpre_b = dpre.astype(bf16)
     expand_bias_grad = jnp.sum(dpre, axis=0)
     dact_part = dot_on(dpre_b, w_expand, 1, 1).astype(bf16).reshape(m, rows, D)
-    (dact_two,) = move(4, ("sum_dp", dact_part))
+    expand_part = dot_on(act_two, dpre_b, 0, 0).astype(bf16).reshape(n, feat, wide)
+    dact_two, expand_grad = move(4, ("sum_dp", dact_part), ("sum_ctx", expand_part))
     out_part = dot_on(hidden_b, w_shrink_t, 1, 1).astype(bf16).reshape(m, rows, D)
 
-    expand_part = dot_on(act_two, dpre_b, 0, 0).astype(bf16).reshape(chips, 2, feat, wide)
-    expand_grad = line_sum(core_sum(expand_part, 1))
     shrink_part = (
-        dot_on(cot_full, hidden_b, 0, 0)
-        .astype(bf16)
-        .reshape(m, fold, cols // fold, fold, hid)
-        .transpose(0, 3, 2, 1, 4)
-        .reshape(m, fold, cols // fold, wide)
-    )
-    shrink_own = line_sum(swap_dp(core_sum(shrink_part, 1)))
-    shrink_grad = (
-        shrink_own.reshape(cols // fold, fold, hid).transpose(1, 0, 2).reshape(cols, hid).T
+        dot_on(cot_full, hidden_b, 0, 0).astype(bf16).reshape(m, fold, cols // fold, wide)
     )
 
     shrink_bias_grad = jnp.sum(cotangent, axis=0)
@@ -1003,21 +1207,21 @@
     dmiddle_b = dmiddle.astype(bf16)
     merge_bias_grad = jnp.sum(dmiddle, axis=0)
     dattended = dot_on(dmiddle_b, w_merge, 1, 1).astype(bf16)
-    datt_main, datt_last = move(
+    merge_part = dot_on(att_own, dmiddle_b, 0, 0).astype(bf16).reshape(n, feat, D)
+    datt_main, datt_last, merge_rows_grad = move(
         5,
         ("swap_ctx", dattended[:, :cut].reshape(rows, n, TILE).transpose(1, 0, 2)),
         ("gather_ctx", jnp.pad(dattended[:, cut:], ((0, 0), (0, TILE - spare)))),
-    )
-    merge_part = dot_on(att_own, dmiddle_b, 0, 0).astype(bf16).reshape(chips, 2, feat, D)
-    merge_rows_grad = line_sum(core_sum(merge_part, 1))
+        ("sum_ctx", merge_part),
+    )
     datt = jnp.concatenate(
         [datt_main.reshape(total, TILE), datt_last.reshape(total, TILE)], axis=1
     )
-    (dqkv,) = attend(
+    dqkv_main, dqkv_last = attend(
         pairs_backward,
         order,
-        (qkv, attended, log_total, datt),
-        [jax.ShapeDtypeStruct((total, 6 * TILE), bf16)],
+        (qkv_main, qkv_last, attended, log_total, datt),
+        [jax.ShapeDtypeStruct((total, 3 * TILE), bf16)] * 2,
         [
             rows_scratch,
             half_scratch,
@@ -1028,22 +1232,25 @@
         ],
         5,
     )
-    lane = lax.broadcasted_iota(jnp.int32, (1, 6 * TILE), 1)
-    counted = ((lane // TILE) % 2 == 0) | (here == 0)
-    w_counted = jnp.where(counted, w_triple, jnp.zeros_like(w_triple))
-    dact_part = dot_on(dqkv, w_counted, 1, 1).astype(bf16).reshape(n, rows, D)
-    dact_one, out_sum = move(6, ("sum_ctx", dact_part), ("sum_dp", out_part))
-    block_out = middle + out_sum + shrink_bias
-    bias_grads = jnp.where(counted[0], jnp.sum(dqkv.astype(f32), axis=0), 0.0)
+    counted = here == 0
+    dqkv_counted = jnp.where(counted, dqkv_last, jnp.zeros_like(dqkv_last))
+    dact_part = dot_on(dqkv_main, w_main, 1, 1) + dot_on(dqkv_counted, w_last, 1, 1)
+    dact_part = dact_part.astype(bf16).reshape(n, rows, D)
+    dact_one, shrink_cross = move(
+        6, ("sum_ctx", dact_part), ("shrink_cross_dp_ctx", shrink_part)
+    )
+    bias_grads = jnp.concatenate(
+        [jnp.sum(dqkv_main.astype(f32), axis=0), jnp.sum(dqkv_counted.astype(f32), axis=0)]
+    )
     gain_one_grad = jnp.sum(dact_one * normed_one, axis=0)
     shift_one_grad = jnp.sum(dact_one, axis=0)
     input_rows = dmiddle + norm_back(dact_one, normed_one, inverse_one, gain_one)
 
     def place(part):
         main = lax.dynamic_update_slice_in_dim(
-            jnp.zeros((cut,), f32), bias_grads[2 * part * TILE :][:TILE], here * TILE, 0
-        )
-        return jnp.concatenate([main, bias_grads[(2 * part + 1) * TILE :][:spare]])
+            jnp.zeros((cut,), f32), bias_grads[part * TILE :][:TILE], here * TILE, 0
+        )
+        return jnp.concatenate([main, bias_grads[(3 + part) * TILE :][:spare]])
 
     expand_bias_all = lax.dynamic_update_slice_in_dim(
         jnp.zeros((m * wide,), f32), expand_bias_grad, seq_here * wide, 0
@@ -1067,13 +1274,16 @@
         ],
         axis=1,
     )
-    triple_part = dot_on(act_one, dqkv, 0, 0).astype(bf16).reshape(D, 3, 2, TILE)
-    triple_main, vector_rows_grad = move(
+    triple_part = dot_on(act_one, dqkv_main, 0, 0).astype(bf16).reshape(n, feat, 3 * TILE)
+    triple_last = dot_on(act_one, dqkv_last, 0, 0).astype(bf16)
+    triple_main, vector_rows_grad, out_sum = move(
         7,
-        ("swap_ctx", triple_part[:, :, 0].reshape(n, feat, 3 * TILE)),
+        ("swap_ctx", triple_part),
         ("sum_ctx", vector_local.reshape(n, feat, -1)),
-    )
-    triple_last = lax.dynamic_slice_in_dim(triple_part[:, :, 1, :spare], here * feat, feat, 0)
+        ("sum_dp", out_part),
+    )
+    triple_last = lax.dynamic_slice_in_dim(triple_last, here * feat, feat, 0)
+    triple_last = triple_last.reshape(feat, 3, TILE)[:, :, :spare]
     triple_rows_grad = jnp.concatenate(
         [
             triple_main.reshape(n, feat, 3, TILE).transpose(1, 2, 0, 3).reshape(feat, 3, cut),
@@ -1082,10 +1292,12 @@
         axis=2,
     )
 
+    block_out = middle + out_sum + shrink_bias
+
     def by_dp(rows_part):
         return rows_part.reshape(feat, m, -1).transpose(1, 0, 2).astype(bf16)
 
-    (last,) = move(
+    last, shrink_sum = move(
         8,
         (
             "sum_dp",
@@ -1093,7 +1305,12 @@
                 [by_dp(triple_rows_grad), by_dp(merge_rows_grad), by_dp(vector_rows_grad)], axis=2
             ),
         ),
-    )
+        ("line_sum_ctx", shrink_cross),
+    )
+    left, right = shrink_sum[:, :hid], shrink_sum[:, hid:]
+    shrink_grad = core_pair(
+        jnp.where(first_core, left, right), trade(jnp.where(first_core, right, left)), 0
+    ).T
     triple_grad = last[:, :tw]
     merge_grad = last[:, tw : tw + mw]
     vector_grad = last[:, tw + mw :]

time: 676 us -> 504 us (0.75)
  waiting for transfers between devices: 110 us -> 0.01 us
  local copies, waits for them, and re-layouts: 164 us -> 54.4 us
  Pallas kernels: 259 us -> 355 us
  starting transfers between devices: 28.9 us -> 2.56 us
  other arithmetic: 65.8 us -> 42.8 us
    ppermute x24 -> x0, waiting for transfers between devices: 107 us -> none  [the longest x18 85.3 us: turn(): return lax.ppermute(x, 'ctx', pairs)]
    pallas_call x9, Pallas kernels: 241 us -> 337 us  [move(): pl.pallas_call(kernel, in_specs=[pl.BlockSpec(memory_space=pltpu.VMEM)] *...]
    reshape x10 -> x2, local copies, waits for them, and re-layouts: 36.9 us -> 3.83 us  [the longest x1 3.8 us: local_pairs(): w_merge = w_merge.reshape(m, D, mw).transpose(1, 0, 2).reshape(D, D)]
    ppermute x24 -> x0, starting transfers between devices: 26.1 us -> none  [the longest x18 18.8 us: turn(): return lax.ppermute(x, 'ctx', pairs)]
    another operation x12 -> x2, local copies, waits for them, and re-layouts: 22.5 us -> 0.01 us  [the longest x4 17.3 us: both_cores(): jnp.stack([x, other], axis)]
    dynamic_update_slice x19 -> x2, local copies, waits for them, and re-layouts: 16 us -> 0.23 us  [place(): lax.dynamic_update_slice_in_dim(jnp.zeros((cut,), f32), bias_grads[part *...]
    transpose x1, other arithmetic: 15.3 us -> 1.23 us  [local_pairs(): shrink_t = shrink_weight.astype(bf16).T]
    squeeze x9 -> x1, local copies, waits for them, and re-layouts: 9.88 us -> 0.01 us  [last_bias(): return jnp.pad(vectors[cut:, column], (0, TILE - spare))]
  transfers between devices with their start and end apart: 30 -> 2, of which waited for: 13 -> 0; matrix products, arithmetic and copies ran while one was open for 18% -> 8% of each run, Pallas kernels for 26% -> 11%
where the time goes in v2:
time: 504 us; the launch traced here: 496 us
  Pallas kernels  355 us (70%)
  local copies, waits for them, and re-layouts  54.4 us (11%)
  other arithmetic  42.8 us (8%)
  matrix products  39.6 us (8%)
    pallas_call x9, Pallas kernels, move(): pl.pallas_call(kernel, in_specs=[pl.BlockSpec(memory_space=pltpu.VMEM)] *...  337 us
    dot_general x16, matrix products, dot_on(): lax.dot_general(left, right, (((left_dim,), (right_dim,)), ((), ())), pre...  39.6 us
    pallas_call x2, Pallas kernels, attend(): pl.pallas_call(kernel, in_specs=[pl.BlockSpec(memory_space=pltpu.SMEM)] +...  17.7 us
    unnamed x153, local copies, waits for them, and re-layouts  11.8 us
    sub x5, other arithmetic, adam_update(): return (weight - learn_rate * direction, moment_new, square_new)  10.6 us
  transfers between devices with their start and end apart: 2, of which 0 were waited for; matrix products, arithmetic and copies ran while one was open for 8% of the time, Pallas kernels for 11%

profile of v2, /device:TPU:9, one launch (start us, length us, event | category | flops | bytes accessed | tf_op | source)
XLA Modules:
  0.0 496.4 jit_solution(17929798478771958977)
XLA Ops:
  0.7 1.2 convert_bitcast_fusion
  3.4 1.3 copy.192
  9.4 53.6 %move_0.1 = (bf16[8,128,1088]{2,1,0:T(8,128)(2,1)}, bf16[8,136,1088]{2,1,0:T(8,128)(2,1)}, bf16[8,136,272]{2,1,0:T(8,128)(2,1)}, bf16[4,136,819]{2,1,0:T(8,128)(2,1)}, bf16[4,128,1088]{2,1,0:T(8,128)(2,1)}) custom-call(bf16[128,1088]{1,0:T(8,128)(2,1)} %fusion.17.refs_0_, bf16[136,1088]{1,0:T(8,128)(2,1)} %convert_element_type.120.refs_1_, ...), custom_call_target="tpu_custom_call" | custom-call | flops 114974400 | bytes 1149744 | tf_op jit(solution)/shard_map/move_0/pallas_call | solution.py:879
  63.0 1.3 slice_bitcast_fusion
  64.3 1.7 slice_bitcast_fusion.2
  71.1 1.4 reshape_reshape.3
  73.7 1.5 reshape.257
  75.2 1.7 copy.198
  76.8 1.5 reshape.226.refs_0_
  80.5 1.4 copy.222
  82.6 1.6 pad_maximum_fusion.6.refs_1_
  84.2 2.1 maximum_select_fusion.1.refs_3_
  86.3 51.4 %move_1.1 = (bf16[8,136,384]{2,1,0:T(8,128)(2,1)}, bf16[8,136,204]{2,1,0:T(8,128)(2,1)}, bf16[4,2,544,272]{3,2,1,0:T(8,128)(2,1)}, bf16[4,2,136,1088]{3,2,1,0:T(8,128)(2,1)}) custom-call(bf16[8,136,384]{2,1,0:T(8,128)(2,1)} %reshape.226.refs_0_, bf16[136,204]{1,0:T(8,128)(2,1)} %pad_maximum_fusion.6.refs_1_, bf16[2,544,272]{2,1,0:T(8,128)(2,1)} %bitcast.149, ...), custom_call_target="tpu_custom_call" | custom-call | flops 177888000 | bytes 1778880 | tf_op jit(solution)/shard_map/move_1/pallas_call | solution.py:879
  137.7 1.1 slice.133
  139.2 2.1 add_convert_fusion
  141.3 2.1 fusion.1
  143.4 3.8 copy.206
  147.4 4.3 add_convert_fusion.2.main_ref
  153.2 2.3 add_convert_fusion.1.last_ref
  155.5 7.9 %shard_map.345 = (bf16[1024,256]{1,0:T(8,128)(2,1)}, f32[1024,128]{1,0:T(8,128)}) custom-call(s32[16]{0:T(128)} %select_reduce_fusion.order_ref, bf16[1024,384]{1,0:T(8,128)(2,1)} %add_convert_fusion.2.main_ref, bf16[1024,384]{1,0:T(8,128)(2,1)} %add_convert_fusion.1.last_ref), custom_call_target="tpu_custom_call" | custom-call | flops 805306368 | bytes 3145728 | tf_op jit(solution)/shard_map/pallas_call | solution.py:1030
  163.4 1.7 slice.111
  165.9 28.8 %move_2.1 = bf16[8,128,128]{2,1,0:T(8,128)(2,1)} custom-call(bf16[8,128,128]{2,1,0:T(8,128)(2,1)} %bitcast.144), custom_call_target="tpu_custom_call" | custom-call | flops 26214400 | bytes 262144 | tf_op jit(solution)/shard_map/move_2/pallas_call | solution.py:879
  194.8 1.1 copy.204
  195.9 1.0 fusion.55
  198.6 18.1 %move_3.1 = bf16[4,128,1088]{2,1,0:T(8,128)(2,1)} custom-call(bf16[128,1088]{1,0:T(8,128)(2,1)} %add_convert_fusion.3.refs_0_), custom_call_target="tpu_custom_call" | custom-call | flops 27852800 | bytes 278528 | tf_op jit(solution)/shard_map/move_3/pallas_call | solution.py:879
  216.9 3.9 convolution_add_fusion.1
  220.8 4.1 fusion.56
  224.9 2.6 convolution_convert_fusion.4
  227.5 3.2 convolution_convert_fusion.1
  230.7 2.5 copy.208
  233.3 35.2 %move_4.1 = (f32[128,1088]{1,0:T(8,128)}, f32[136,1088]{1,0:T(8,128)}) custom-call(bf16[4,128,1088]{2,1,0:T(8,128)(2,1)} %bitcast.130, bf16[8,136,1088]{2,1,0:T(8,128)(2,1)} %bitcast.137), custom_call_target="tpu_custom_call" | custom-call | flops 348160000 | bytes 3481600 | tf_op jit(solution)/shard_map/move_4/pallas_call | solution.py:879
  268.5 1.5 multiply_reduce_fusion.1
  270.0 1.7 fusion.52
  273.1 2.3 convolution_convert_fusion.2
  275.4 3.3 convolution_convert_fusion
  279.3 51.4 %move_5.1 = (bf16[8,128,128]{2,1,0:T(8,128)(2,1)}, bf16[8,128,128]{2,1,0:T(8,128)(2,1)}, f32[136,1088]{1,0:T(8,128)}) custom-call(bf16[8,128,128]{2,1,0:T(8,128)(2,1)} %bitcast_bitcast_fusion.refs_0_, bf16[128,128]{1,0:T(8,128)(2,1)} %pad.13.refs_1_, bf16[8,136,1088]{2,1,0:T(8,128)(2,1)} %bitcast.128), custom_call_target="tpu_custom_call" | custom-call | flops 266240000 | bytes 2662400 | tf_op jit(solution)/shard_map/move_5/pallas_call | solution.py:879
  330.7 1.9 pad_maximum_fusion.1.dout_ref
  332.6 9.8 %shard_map.346 = (bf16[1024,384]{1,0:T(8,128)(2,1)}, bf16[1024,384]{1,0:T(8,128)(2,1)}) custom-call(s32[16]{0:T(128)} %select_reduce_fusion.order_ref, bf16[1024,384]{1,0:T(8,128)(2,1)} %add_convert_fusion.2.main_ref, bf16[1024,384]{1,0:T(8,128)(2,1)} %add_convert_fusion.1.last_ref, bf16[1024,256]{1,0:T(8,128)(2,1)} %get-tuple-element.52.out_ref, ...), custom_call_target="tpu_custom_call" | custom-call | flops 2013265920 | bytes 3145728 | tf_op jit(solution)/shard_map/pallas_call | solution.py:1030
  342.4 2.6 fusion.57
  345.1 2.3 convolution_convert_fusion.5
  348.2 2.8 convolution_convert_fusion.3
  351.0 2.3 fusion.58
  353.5 1.4 fusion.2
  354.9 2.6 copy.211
  357.5 37.7 %move_6.1 = (f32[128,1088]{1,0:T(8,128)}, bf16[4,136,1088]{2,1,0:T(8,128)(2,1)}) custom-call(bf16[8,128,1088]{2,1,0:T(8,128)(2,1)} %bitcast.129, bf16[4,2,136,1088]{3,2,1,0:T(8,128)(2,1)} %bitcast.136), custom_call_target="tpu_custom_call" | custom-call | flops 459571200 | bytes 4595712 | tf_op jit(solution)/shard_map/move_6/pallas_call | solution.py:879
  395.2 1.4 multiply_reduce_fusion
  399.5 1.1 copy.213.refs_1_
  400.6 1.4 copy.212
  402.0 29.6 %move_7.1 = (bf16[8,136,384]{2,1,0:T(8,128)(2,1)}, f32[136,12]{1,0:T(8,128)}, f32[128,1088]{1,0:T(8,128)}) custom-call(bf16[8,136,384]{2,1,0:T(8,128)(2,1)} %bitcast.148, f32[8,136,12]{2,1,0:T(8,128)} %copy.213.refs_1_, bf16[4,128,1088]{2,1,0:T(8,128)(2,1)} %bitcast.131), custom_call_target="tpu_custom_call" | custom-call | flops 200192000 | bytes 2001920 | tf_op jit(solution)/shard_map/move_7/pallas_call | solution.py:879
  431.6 1.4 add_bitcast_fusion
  433.1 1.0 copy.225
  434.1 1.0 copy.226
  436.1 2.5 reshape.252
  439.9 1.4 reshape.255
  442.5 2.1 concatenate.86.refs_0_
  444.7 31.3 %move_8.1 = (f32[136,1091]{1,0:T(8,128)}, f32[136,1088]{1,0:T(8,128)}) custom-call(bf16[4,136,1091]{2,1,0:T(8,128)(2,1)} %concatenate.86.refs_0_, bf16[4,136,1088]{2,1,0:T(8,128)(2,1)} %get-tuple-element.68.refs_1_), custom_call_target="tpu_custom_call" | custom-call | flops 237075200 | bytes 2370752 | tf_op jit(solution)/shard_map/move_8/pallas_call | solution.py:879
  476.0 2.1 slice_select_fusion
  478.1 1.9 collective-permute-start.1
  480.0 1.6 multiply_subtract_fusion.4
  481.6 1.6 copy.227
  485.2 2.1 multiply_subtract_fusion.3
  487.3 2.7 multiply_subtract_fusion.1
  490.1 1.4 multiply_subtract_fusion.2
  492.3 2.8 multiply_subtract_fusion
  (248 shorter events, 32.6 us)
Async XLA Ops:
  0.7 4.0 copy-start.16
  0.7 5.3 %copy-start.10 = (f32[136,1088]{1,0:T(8,128)S(1)}, f32[136,1088]{1,0:T(8,128)}, u32[]{:S(2)}) copy-start(f32[136,1088]{1,0:T(8,128)} %param.23) | copy-start | bytes 1775620
  2.7 4.0 copy-start.27
  2.7 4.7 copy-start.42
  2.7 4.8 copy-start.19
  2.7 81.5 %collective-permute-start = (bf16[136,544]{1,0:T(8,128)(2,1)}, bf16[136,544]{1,0:T(8,128)(2,1)}, u32[]{:S(2)}, u32[]{:S(2)}) collective-permute-start(bf16[136,544]{1,0:T(8,128)(2,1)} %get-tuple-element.220), channel_id=1, source_target_pairs={{0,1},{1,0},{2,3},{3,2},{4,5},{5,4},{6,7},{7,6},{8,9},{9,8},{10,11... | collective-permute-start | bytes 443912 | tf_op jit(solution)/shard_map/ppermute | solution.py:1045
  4.7 2.9 copy-start.17
  4.9 2.9 copy-start.43
  5.1 1.6 copy-start.46
  7.8 56.5 %copy-start.5 = (f32[1,128,1088]{2,1,0:T(8,128)}, f32[1,128,1088]{2,1,0:T(8,128)S(1)}, u32[]{:S(2)}) copy-start(f32[1,128,1088]{2,1,0:T(8,128)S(1)} %copy.195) | copy-start | bytes 1671172
  7.8 61.0 %copy-start.55 = (s32[8,2]{0,1:T(2,128)S(1)}, s32[8,2]{0,1:T(2,128)}, u32[]{:S(2)}) copy-start(s32[8,2]{0,1:T(2,128)} %param.20) | copy-start | bytes 196
  8.6 61.0 %copy-start.48 = (f32[136,3]{0,1:T(4,128)S(1)}, f32[136,3]{0,1:T(4,128)}, u32[]{:S(2)}) copy-start(f32[136,3]{0,1:T(4,128)} %param.30) | copy-start | bytes 4900
  8.7 61.6 %copy-start.49 = (f32[136,3]{0,1:T(4,128)S(1)}, f32[136,3]{0,1:T(4,128)}, u32[]{:S(2)}) copy-start(f32[136,3]{0,1:T(4,128)} %param.35) | copy-start | bytes 4900
  72.5 2.6 copy-start.6
  75.2 3.2 copy-start.33
  75.2 3.5 slice-start
  75.2 4.4 copy-start.18
  79.5 59.6 %copy-start.4 = (bf16[8,128,1088]{2,1,0:T(8,128)(2,1)S(1)}, bf16[8,128,1088]{2,1,0:T(8,128)(2,1)}, u32[]{:S(2)}) copy-start(bf16[8,128,1088]{2,1,0:T(8,128)(2,1)} %get-tuple-element.47) | copy-start | bytes 6684676
  147.3 4.4 copy-start.39
  147.3 4.4 copy-start.51
  147.3 4.4 copy-start.52
  147.4 4.4 copy-start.53
  147.4 4.4 copy-start.54
  147.4 4.4 copy-start.61
  147.4 4.4 copy-start.62
  147.4 5.8 %copy-start.14 = (bf16[1024,1088]{1,0:T(8,128)(2,1)S(1)}, bf16[1024,1088]{1,0:T(8,128)(2,1)}, u32[]{:S(2)}) copy-start(bf16[1024,1088]{1,0:T(8,128)(2,1)} %fusion.1) | copy-start | bytes 6684676
  216.9 3.9 copy-start.57
  216.9 3.9 copy-start.59
  220.7 4.1 copy-start.63
  220.8 4.1 copy-start.56
  224.9 2.7 copy-start.21
  272.3 3.1 copy-start.60
  272.3 3.1 copy-start.64
  332.6 9.8 %copy-start.24 = (bf16[8,136,384]{2,1,0:T(8,128)(2,1)S(1)}, bf16[8,136,384]{2,1,0:T(8,128)(2,1)}, u32[]{:S(2)}) copy-start(bf16[8,136,384]{2,1,0:T(8,128)(2,1)} %get-tuple-element.51) | copy-start | bytes 2506756
  342.4 2.6 copy-start.7
  342.4 2.7 copy-start.15
  345.1 3.1 copy-start.58
  345.1 3.1 copy-start.65
  348.2 2.8 copy-start.8
  351.0 2.6 copy-start.26
  357.5 37.7 %copy-start.44 = (f32[128]{0:T(128)S(1)}, f32[128]{0:T(128)}, u32[]{:S(2)}) copy-start(f32[128]{0:T(128)} %copy-done.43) | copy-start | bytes 1540
  357.5 37.7 %copy-start.47 = (f32[128]{0:T(128)S(1)}, f32[128]{0:T(128)}, u32[]{:S(2)}) copy-start(f32[128]{0:T(128)} %copy-done.46) | copy-start | bytes 1540
  357.5 40.4 %copy-start.50 = (f32[384]{0:T(512)S(1)}, f32[384]{0:T(512)}, u32[]{:S(2)}) copy-start(f32[384]{0:T(512)} %convert_reduce_fusion.1) | copy-start | bytes 4612
  357.5 41.1 %copy-start.45 = (f32[1088]{0:T(1024)S(1)}, f32[1088]{0:T(1024)}, u32[]{:S(2)}) copy-start(f32[1088]{0:T(1024)} %get-tuple-element.231) | copy-start | bytes 13060
  357.5 41.9 %copy-start.41 = (f32[8,136,1]{1,0,2:T(8,128)S(1)}, f32[8,136,1]{1,0,2:T(8,128)}, u32[]{:S(2)}) copy-start(f32[8,136,1]{1,0,2:T(8,128)} %concatenate.82) | copy-start | bytes 13060
  395.2 5.4 %copy-start.22 = (bf16[512,1088]{0,1:T(8,128)(2,1)S(1)}, bf16[512,1088]{0,1:T(8,128)(2,1)}, u32[]{:S(2)}) copy-start(bf16[512,1088]{0,1:T(8,128)(2,1)} %convolution_convert_fusion.3) | copy-start | bytes 3342340
  400.6 31.1 %copy-start.1 = (f32[128,1088]{1,0:T(8,128)S(1)}, f32[128,1088]{1,0:T(8,128)}, u32[]{:S(2)}) copy-start(f32[128,1088]{1,0:T(8,128)} %copy-done) | copy-start | bytes 1671172
  400.6 31.1 %copy-start.3 = (f32[128,1088]{1,0:T(8,128)S(1)}, f32[128,1088]{1,0:T(8,128)}, u32[]{:S(2)}) copy-start(f32[128,1088]{1,0:T(8,128)} %copy-done.2) | copy-start | bytes 1671172
  400.6 31.1 %copy-start.13 = (f32[128,1088]{1,0:T(8,128)S(1)}, f32[128,1088]{1,0:T(8,128)}, u32[]{:S(2)}) copy-start(f32[128,1088]{1,0:T(8,128)} %get-tuple-element.63) | copy-start | bytes 1671172
  439.9 1.6 copy-start.32
  444.7 35.3 %copy-start.36 = (f32[136,3]{1,0:T(8,128)S(1)}, f32[136,3]{1,0:T(8,128)}, u32[]{:S(2)}) copy-start(f32[136,3]{1,0:T(8,128)} %copy.224) | copy-start | bytes 4900
  444.7 35.3 %copy-start.37 = (f32[136,3]{1,0:T(8,128)S(1)}, f32[136,3]{1,0:T(8,128)}, u32[]{:S(2)}) copy-start(f32[136,3]{1,0:T(8,128)} %copy.222) | copy-start | bytes 4900
  444.7 35.3 %copy-start.38 = (f32[136,3]{1,0:T(8,128)S(1)}, f32[136,3]{1,0:T(8,128)}, u32[]{:S(2)}) copy-start(f32[136,3]{1,0:T(8,128)} %copy.223) | copy-start | bytes 4900
  444.7 40.5 %copy-start.28 = (f32[136,272]{1,0:T(8,128)S(1)}, f32[136,272]{1,0:T(8,128)}, u32[]{:S(2)}) copy-start(f32[136,272]{1,0:T(8,128)} %param.22) | copy-start | bytes 443908
  476.0 9.2 %copy-start.23 = (f32[136,1091]{1,0:T(8,128)S(1)}, f32[136,1091]{1,0:T(8,128)}, u32[]{:S(2)}) copy-start(f32[136,1091]{1,0:T(8,128)} %get-tuple-element.69) | copy-start | bytes 1780516
  476.0 11.3 %copy-start.11 = (f32[136,1088]{1,0:T(8,128)S(1)}, f32[136,1088]{1,0:T(8,128)}, u32[]{:S(2)}) copy-start(f32[136,1088]{1,0:T(8,128)} %param.23) | copy-start | bytes 1775620
  476.0 11.3 %copy-start.12 = (f32[136,1088]{1,0:T(8,128)S(1)}, f32[136,1088]{1,0:T(8,128)}, u32[]{:S(2)}) copy-start(f32[136,1088]{1,0:T(8,128)} %get-tuple-element.263) | copy-start | bytes 1775620
  476.0 11.3 %copy-start.31 = (f32[136,1088]{1,0:T(8,128)S(1)}, f32[136,1088]{1,0:T(8,128)}, u32[]{:S(2)}) copy-start(f32[136,1088]{1,0:T(8,128)} %param.28) | copy-start | bytes 1775620
  478.1 13.3 %collective-permute-start.1 = (f32[136,544]{1,0:T(8,128)}, f32[136,544]{1,0:T(8,128)}, u32[]{:S(2)}, u32[]{:S(2)}) collective-permute-start(f32[136,544]{1,0:T(8,128)} %get-tuple-element.217), channel_id=1, source_target_pairs={{0,1},{1,0},{2,3},{3,2},{4,5},{5,4},{6,7},{7,6},{8,9},{9,8},{10,11... | collective-permute-start | bytes 887816 | tf_op jit(solution)/shard_map/ppermute | solution.py:1045
  487.3 2.8 copy-start.20
  487.3 2.8 copy-start.34
  487.3 2.8 copy-start.35
  490.1 2.0 copy-start.29
  490.1 2.2 copy-start.30
  (5 other events, 5.4 us)

commit v3 on v2

--- a/solution.py
+++ b/solution.py
@@ -1107,17 +1107,15 @@
     )
     normed_one, inverse_one = layer_norm(stream)
     cot_b = cotangent.astype(bf16)
-    normed_full, w_expand, merge_line, columns, cot_full = move(
+    normed_full, merge_line, columns, cot_full = move(
         0,
         ("gather_ctx", normed_one.astype(bf16)),
-        ("gather_ctx", w_expand_own),
         ("gather_ctx", merge_weight.astype(bf16)),
         ("gather_dp", packed),
         ("gather_dp", cot_b),
     )
     normed_full = normed_full.reshape(total, D)
     cot_full = cot_full.reshape(m * rows, D)
-    w_expand = w_expand.reshape(D, wide)
 
     def take(start, width):
         return columns[:, :, start : start + width].transpose(1, 0, 2).reshape(feat, m * width)
@@ -1184,7 +1182,12 @@
     )
     middle = stream + dot_on(att_own, w_merge, 1, 0) + merge_bias
     normed_two, inverse_two = layer_norm(middle)
-    (act_two,) = move(3, ("gather_dp", (normed_two * gain_two + shift_two).astype(bf16)))
+    act_two, w_expand = move(
+        3,
+        ("gather_dp", (normed_two * gain_two + shift_two).astype(bf16)),
+        ("gather_ctx", w_expand_own),
+    )
+    w_expand = w_expand.reshape(D, wide)
     act_two = act_two.reshape(m * rows, D)
     pre_act = dot_on(act_two, w_expand, 1, 0) + expand_bias
     hidden_b = gelu_value(pre_act).astype(bf16)

time: 504 us -> 497 us (0.986)
  Pallas kernels: 355 us -> 348 us
    pallas_call x9, Pallas kernels: 337 us -> 330 us  [move(): pl.pallas_call(kernel, in_specs=[pl.BlockSpec(memory_space=pltpu.VMEM)] *...]
  transfers between devices with their start and end apart: 2 -> 2, of which waited for: 0 -> 0; matrix products, arithmetic and copies ran while one was open for 8% -> 8% of each run, Pallas kernels for 11% -> 7%
where the time goes in v3:
time: 497 us; the launch traced here: 490 us
  Pallas kernels  348 us (70%)
  local copies, waits for them, and re-layouts  54.6 us (11%)
  other arithmetic  43.7 us (9%)
  matrix products  39.5 us (8%)
    pallas_call x9, Pallas kernels, move(): pl.pallas_call(kernel, in_specs=[pl.BlockSpec(memory_space=pltpu.VMEM)] *...  330 us
    dot_general x16, matrix products, dot_on(): lax.dot_general(left, right, (((left_dim,), (right_dim,)), ((), ())), pre...  39.5 us
    pallas_call x2, Pallas kernels, attend(): pl.pallas_call(kernel, in_specs=[pl.BlockSpec(memory_space=pltpu.SMEM)] +...  17.7 us
    unnamed x153, local copies, waits for them, and re-layouts  12.1 us
    sub x5, other arithmetic, adam_update(): return (weight - learn_rate * direction, moment_new, square_new)  10.6 us
  transfers between devices with their start and end apart: 2, of which 0 were waited for; matrix products, arithmetic and copies ran while one was open for 8% of the time, Pallas kernels for 7%

profile of v3, /device:TPU:9, one launch (start us, length us, event | category | flops | bytes accessed | tf_op | source)
XLA Modules:
  0.0 489.6 jit_solution(16596254075681923262)
XLA Ops:
  0.7 1.2 convert_bitcast_fusion
  3.4 1.3 copy.192
  8.6 31.8 %move_0.1 = (bf16[8,128,1088]{2,1,0:T(8,128)(2,1)}, bf16[8,136,272]{2,1,0:T(8,128)(2,1)}, bf16[4,136,819]{2,1,0:T(8,128)(2,1)}, bf16[4,128,1088]{2,1,0:T(8,128)(2,1)}) custom-call(bf16[128,1088]{1,0:T(8,128)(2,1)} %fusion.17.refs_0_, bf16[136,272]{1,0:T(8,128)(2,1)} %convert_element_type.120.refs_1_, bf16[136,819]{1,0:T(8,128)(2,1)} %pad_maximum_fusion.3.refs_2_, ...), custom_call_target="tpu_custom_call" | custom-call | flops 85380800 | bytes 853808 | tf_op jit(solution)/shard_map/move_0/pallas_call | solution.py:879
  40.4 1.3 slice_bitcast_fusion
  41.7 1.7 slice_bitcast_fusion.2
  48.5 1.4 reshape_reshape.3
  51.1 1.5 reshape.257
  52.6 1.7 copy.198
  54.3 1.5 reshape.226.refs_0_
  58.7 1.4 copy.222
  60.8 1.6 pad_maximum_fusion.6.refs_1_
  62.4 2.1 maximum_select_fusion.1.refs_3_
  64.5 51.9 %move_1.1 = (bf16[8,136,384]{2,1,0:T(8,128)(2,1)}, bf16[8,136,204]{2,1,0:T(8,128)(2,1)}, bf16[4,2,544,272]{3,2,1,0:T(8,128)(2,1)}, bf16[4,2,136,1088]{3,2,1,0:T(8,128)(2,1)}) custom-call(bf16[8,136,384]{2,1,0:T(8,128)(2,1)} %reshape.226.refs_0_, bf16[136,204]{1,0:T(8,128)(2,1)} %pad_maximum_fusion.6.refs_1_, bf16[2,544,272]{2,1,0:T(8,128)(2,1)} %bitcast.147, ...), custom_call_target="tpu_custom_call" | custom-call | flops 177888000 | bytes 1778880 | tf_op jit(solution)/shard_map/move_1/pallas_call | solution.py:879
  116.4 1.1 slice.133
  117.8 2.1 add_convert_fusion
  119.9 2.0 fusion.1
  121.9 3.8 copy.206
  126.0 4.4 add_convert_fusion.2.main_ref
  131.9 2.3 add_convert_fusion.1.last_ref
  134.2 7.9 %shard_map.345 = (bf16[1024,256]{1,0:T(8,128)(2,1)}, f32[1024,128]{1,0:T(8,128)}) custom-call(s32[16]{0:T(128)} %select_reduce_fusion.order_ref, bf16[1024,384]{1,0:T(8,128)(2,1)} %add_convert_fusion.2.main_ref, bf16[1024,384]{1,0:T(8,128)(2,1)} %add_convert_fusion.1.last_ref), custom_call_target="tpu_custom_call" | custom-call | flops 805306368 | bytes 3145728 | tf_op jit(solution)/shard_map/pallas_call | solution.py:1030
  142.1 1.7 slice.111
  144.6 28.8 %move_2.1 = bf16[8,128,128]{2,1,0:T(8,128)(2,1)} custom-call(bf16[8,128,128]{2,1,0:T(8,128)(2,1)} %bitcast.142), custom_call_target="tpu_custom_call" | custom-call | flops 26214400 | bytes 262144 | tf_op jit(solution)/shard_map/move_2/pallas_call | solution.py:879
  173.4 1.1 copy.204
  174.6 1.0 fusion.55
  176.7 2.0 add_convert_fusion.3.refs_0_
  178.7 26.0 %move_3.1 = (bf16[4,128,1088]{2,1,0:T(8,128)(2,1)}, bf16[8,136,1088]{2,1,0:T(8,128)(2,1)}) custom-call(bf16[128,1088]{1,0:T(8,128)(2,1)} %add_convert_fusion.3.refs_0_, bf16[136,1088]{1,0:T(8,128)(2,1)} %convert_element_type.136.refs_1_), custom_call_target="tpu_custom_call" | custom-call | flops 57446400 | bytes 574464 | tf_op jit(solution)/shard_map/move_3/pallas_call | solution.py:879
  204.8 3.9 convolution_add_fusion.1
  208.7 4.1 fusion.56
  212.8 2.6 convolution_convert_fusion.4
  215.4 3.2 convolution_convert_fusion.1
  218.6 2.5 copy.208
  221.2 40.2 %move_4.1 = (f32[128,1088]{1,0:T(8,128)}, f32[136,1088]{1,0:T(8,128)}) custom-call(bf16[4,128,1088]{2,1,0:T(8,128)(2,1)} %bitcast.130, bf16[8,136,1088]{2,1,0:T(8,128)(2,1)} %bitcast.137), custom_call_target="tpu_custom_call" | custom-call | flops 348160000 | bytes 3481600 | tf_op jit(solution)/shard_map/move_4/pallas_call | solution.py:879
  261.3 1.5 multiply_reduce_fusion.1
  262.9 1.7 fusion.52
  265.9 2.2 convolution_convert_fusion.2
  268.2 3.3 convolution_convert_fusion
  272.1 51.1 %move_5.1 = (bf16[8,128,128]{2,1,0:T(8,128)(2,1)}, bf16[8,128,128]{2,1,0:T(8,128)(2,1)}, f32[136,1088]{1,0:T(8,128)}) custom-call(bf16[8,128,128]{2,1,0:T(8,128)(2,1)} %bitcast_bitcast_fusion.refs_0_, bf16[128,128]{1,0:T(8,128)(2,1)} %pad.13.refs_1_, bf16[8,136,1088]{2,1,0:T(8,128)(2,1)} %bitcast.128), custom_call_target="tpu_custom_call" | custom-call | flops 266240000 | bytes 2662400 | tf_op jit(solution)/shard_map/move_5/pallas_call | solution.py:879
  323.1 1.9 pad_maximum_fusion.1.dout_ref
  325.0 9.8 %shard_map.346 = (bf16[1024,384]{1,0:T(8,128)(2,1)}, bf16[1024,384]{1,0:T(8,128)(2,1)}) custom-call(s32[16]{0:T(128)} %select_reduce_fusion.order_ref, bf16[1024,384]{1,0:T(8,128)(2,1)} %add_convert_fusion.2.main_ref, bf16[1024,384]{1,0:T(8,128)(2,1)} %add_convert_fusion.1.last_ref, bf16[1024,256]{1,0:T(8,128)(2,1)} %get-tuple-element.53.out_ref, ...), custom_call_target="tpu_custom_call" | custom-call | flops 2013265920 | bytes 3145728 | tf_op jit(solution)/shard_map/pallas_call | solution.py:1030
  334.9 2.6 fusion.57
  337.5 2.3 convolution_convert_fusion.5
  340.6 2.8 convolution_convert_fusion.3
  343.3 2.3 fusion.58
  345.9 1.4 fusion.2
  347.2 2.6 copy.211
  349.8 37.6 %move_6.1 = (f32[128,1088]{1,0:T(8,128)}, bf16[4,136,1088]{2,1,0:T(8,128)(2,1)}) custom-call(bf16[8,128,1088]{2,1,0:T(8,128)(2,1)} %bitcast.129, bf16[4,2,136,1088]{3,2,1,0:T(8,128)(2,1)} %bitcast.136), custom_call_target="tpu_custom_call" | custom-call | flops 459571200 | bytes 4595712 | tf_op jit(solution)/shard_map/move_6/pallas_call | solution.py:879
  387.5 1.4 multiply_reduce_fusion
  391.7 1.1 copy.213.refs_1_
  392.8 1.4 copy.212
  394.2 29.8 %move_7.1 = (bf16[8,136,384]{2,1,0:T(8,128)(2,1)}, f32[136,12]{1,0:T(8,128)}, f32[128,1088]{1,0:T(8,128)}) custom-call(bf16[8,136,384]{2,1,0:T(8,128)(2,1)} %bitcast.146, f32[8,136,12]{2,1,0:T(8,128)} %copy.213.refs_1_, bf16[4,128,1088]{2,1,0:T(8,128)(2,1)} %bitcast.131), custom_call_target="tpu_custom_call" | custom-call | flops 200192000 | bytes 2001920 | tf_op jit(solution)/shard_map/move_7/pallas_call | solution.py:879
  424.1 1.4 add_bitcast_fusion
  425.5 1.0 copy.225
  428.5 2.5 reshape.252
  432.4 1.4 reshape.255
  435.0 2.1 concatenate.86.refs_0_
  437.1 32.7 %move_8.1 = (f32[136,1091]{1,0:T(8,128)}, f32[136,1088]{1,0:T(8,128)}) custom-call(bf16[4,136,1091]{2,1,0:T(8,128)(2,1)} %concatenate.86.refs_0_, bf16[4,136,1088]{2,1,0:T(8,128)(2,1)} %get-tuple-element.70.refs_1_), custom_call_target="tpu_custom_call" | custom-call | flops 237075200 | bytes 2370752 | tf_op jit(solution)/shard_map/move_8/pallas_call | solution.py:879
  469.9 2.1 slice_select_fusion
  472.0 1.2 collective-permute-start.1
  473.2 1.6 multiply_subtract_fusion.4
  474.8 1.6 copy.227
  478.4 2.1 multiply_subtract_fusion.3
  480.5 2.7 multiply_subtract_fusion.1
  483.3 1.4 multiply_subtract_fusion.2
  485.5 2.8 multiply_subtract_fusion
  (248 shorter events, 32.9 us)
Async XLA Ops:
  0.7 4.0 copy-start.16
  0.7 5.2 %copy-start.26 = (f32[136,272]{1,0:T(8,128)S(1)}, f32[136,272]{1,0:T(8,128)}, u32[]{:S(2)}) copy-start(f32[136,272]{1,0:T(8,128)} %param.22) | copy-start | bytes 443908
  1.9 4.7 copy-start.41
  1.9 4.8 copy-start.19
  2.7 4.1 copy-start.17
  2.7 59.7 %collective-permute-start = (bf16[136,544]{1,0:T(8,128)(2,1)}, bf16[136,544]{1,0:T(8,128)(2,1)}, u32[]{:S(2)}, u32[]{:S(2)}) collective-permute-start(bf16[136,544]{1,0:T(8,128)(2,1)} %get-tuple-element.222), channel_id=1, source_target_pairs={{0,1},{1,0},{2,3},{3,2},{4,5},{5,4},{6,7},{7,6},{8,9},{9,8},{10,11... | collective-permute-start | bytes 443912 | tf_op jit(solution)/shard_map/ppermute | solution.py:1045
  4.8 1.8 copy-start.42
  7.0 36.4 %copy-start.5 = (f32[1,128,1088]{2,1,0:T(8,128)}, f32[1,128,1088]{2,1,0:T(8,128)S(1)}, u32[]{:S(2)}) copy-start(f32[1,128,1088]{2,1,0:T(8,128)S(1)} %copy.195) | copy-start | bytes 1671172
  7.0 39.2 %copy-start.54 = (s32[8,2]{0,1:T(2,128)S(1)}, s32[8,2]{0,1:T(2,128)}, u32[]{:S(2)}) copy-start(s32[8,2]{0,1:T(2,128)} %param.20) | copy-start | bytes 196
  7.0 40.0 %copy-start.47 = (f32[136,3]{0,1:T(4,128)S(1)}, f32[136,3]{0,1:T(4,128)}, u32[]{:S(2)}) copy-start(f32[136,3]{0,1:T(4,128)} %param.30) | copy-start | bytes 4900
  7.0 40.6 %copy-start.48 = (f32[136,3]{0,1:T(4,128)S(1)}, f32[136,3]{0,1:T(4,128)}, u32[]{:S(2)}) copy-start(f32[136,3]{0,1:T(4,128)} %param.35) | copy-start | bytes 4900
  49.9 2.6 copy-start.6
  52.6 3.2 copy-start.32
  52.6 3.5 slice-start
  52.6 4.4 copy-start.10
  54.2 3.5 copy-start.18
  57.7 60.1 %copy-start.4 = (bf16[8,128,1088]{2,1,0:T(8,128)(2,1)S(1)}, bf16[8,128,1088]{2,1,0:T(8,128)(2,1)}, u32[]{:S(2)}) copy-start(bf16[8,128,1088]{2,1,0:T(8,128)(2,1)} %get-tuple-element.48) | copy-start | bytes 6684676
  125.9 4.5 copy-start.38
  125.9 4.5 copy-start.50
  125.9 4.5 copy-start.51
  125.9 4.5 copy-start.52
  125.9 4.5 copy-start.53
  126.0 4.5 copy-start.61
  126.0 4.5 copy-start.62
  126.0 5.9 %copy-start.14 = (bf16[1024,1088]{1,0:T(8,128)(2,1)S(1)}, bf16[1024,1088]{1,0:T(8,128)(2,1)}, u32[]{:S(2)}) copy-start(bf16[1024,1088]{1,0:T(8,128)(2,1)} %fusion.1) | copy-start | bytes 6684676
  204.8 3.9 copy-start.55
  204.8 3.9 copy-start.58
  208.7 4.1 copy-start.63
  208.7 4.1 copy-start.57
  212.8 2.6 copy-start.60
  265.1 3.0 copy-start.59
  265.1 3.0 copy-start.64
  325.0 9.9 %copy-start.23 = (bf16[8,136,384]{2,1,0:T(8,128)(2,1)S(1)}, bf16[8,136,384]{2,1,0:T(8,128)(2,1)}, u32[]{:S(2)}) copy-start(bf16[8,136,384]{2,1,0:T(8,128)(2,1)} %get-tuple-element.52) | copy-start | bytes 2506756
  334.9 2.6 copy-start.7
  334.9 2.7 copy-start.15
  337.5 3.0 copy-start.56
  337.5 3.0 copy-start.65
  340.6 2.8 copy-start.8
  343.3 2.5 copy-start.25
  349.8 37.6 %copy-start.43 = (f32[128]{0:T(128)S(1)}, f32[128]{0:T(128)}, u32[]{:S(2)}) copy-start(f32[128]{0:T(128)} %copy-done.42) | copy-start | bytes 1540
  349.8 37.6 %copy-start.46 = (f32[128]{0:T(128)S(1)}, f32[128]{0:T(128)}, u32[]{:S(2)}) copy-start(f32[128]{0:T(128)} %copy-done.45) | copy-start | bytes 1540
  349.8 40.3 %copy-start.49 = (f32[384]{0:T(512)S(1)}, f32[384]{0:T(512)}, u32[]{:S(2)}) copy-start(f32[384]{0:T(512)} %convert_reduce_fusion.1) | copy-start | bytes 4612
  349.8 41.0 %copy-start.44 = (f32[1088]{0:T(1024)S(1)}, f32[1088]{0:T(1024)}, u32[]{:S(2)}) copy-start(f32[1088]{0:T(1024)} %get-tuple-element.233) | copy-start | bytes 13060
  349.8 41.8 %copy-start.40 = (f32[8,136,1]{1,0,2:T(8,128)S(1)}, f32[8,136,1]{1,0,2:T(8,128)}, u32[]{:S(2)}) copy-start(f32[8,136,1]{1,0,2:T(8,128)} %concatenate.82) | copy-start | bytes 13060
  387.4 5.4 %copy-start.21 = (bf16[512,1088]{0,1:T(8,128)(2,1)S(1)}, bf16[512,1088]{0,1:T(8,128)(2,1)}, u32[]{:S(2)}) copy-start(bf16[512,1088]{0,1:T(8,128)(2,1)} %convolution_convert_fusion.3) | copy-start | bytes 3342340
  392.8 31.3 %copy-start.1 = (f32[128,1088]{1,0:T(8,128)S(1)}, f32[128,1088]{1,0:T(8,128)}, u32[]{:S(2)}) copy-start(f32[128,1088]{1,0:T(8,128)} %copy-done) | copy-start | bytes 1671172
  392.8 31.3 %copy-start.3 = (f32[128,1088]{1,0:T(8,128)S(1)}, f32[128,1088]{1,0:T(8,128)}, u32[]{:S(2)}) copy-start(f32[128,1088]{1,0:T(8,128)} %copy-done.2) | copy-start | bytes 1671172
  392.8 31.3 %copy-start.13 = (f32[128,1088]{1,0:T(8,128)S(1)}, f32[128,1088]{1,0:T(8,128)}, u32[]{:S(2)}) copy-start(f32[128,1088]{1,0:T(8,128)} %get-tuple-element.65) | copy-start | bytes 1671172
  432.3 1.6 copy-start.31
  437.1 36.1 %copy-start.35 = (f32[136,3]{1,0:T(8,128)S(1)}, f32[136,3]{1,0:T(8,128)}, u32[]{:S(2)}) copy-start(f32[136,3]{1,0:T(8,128)} %copy.224) | copy-start | bytes 4900
  437.1 36.1 %copy-start.36 = (f32[136,3]{1,0:T(8,128)S(1)}, f32[136,3]{1,0:T(8,128)}, u32[]{:S(2)}) copy-start(f32[136,3]{1,0:T(8,128)} %copy.222) | copy-start | bytes 4900
  437.1 36.1 %copy-start.37 = (f32[136,3]{1,0:T(8,128)S(1)}, f32[136,3]{1,0:T(8,128)}, u32[]{:S(2)}) copy-start(f32[136,3]{1,0:T(8,128)} %copy.223) | copy-start | bytes 4900
  437.1 41.3 %copy-start.27 = (f32[136,272]{1,0:T(8,128)S(1)}, f32[136,272]{1,0:T(8,128)}, u32[]{:S(2)}) copy-start(f32[136,272]{1,0:T(8,128)} %param.22) | copy-start | bytes 443908
  469.9 8.5 %copy-start.22 = (f32[136,1091]{1,0:T(8,128)S(1)}, f32[136,1091]{1,0:T(8,128)}, u32[]{:S(2)}) copy-start(f32[136,1091]{1,0:T(8,128)} %get-tuple-element.71) | copy-start | bytes 1780516
  469.9 10.6 %copy-start.11 = (f32[136,1088]{1,0:T(8,128)S(1)}, f32[136,1088]{1,0:T(8,128)}, u32[]{:S(2)}) copy-start(f32[136,1088]{1,0:T(8,128)} %param.23) | copy-start | bytes 1775620
  469.9 10.6 %copy-start.12 = (f32[136,1088]{1,0:T(8,128)S(1)}, f32[136,1088]{1,0:T(8,128)}, u32[]{:S(2)}) copy-start(f32[136,1088]{1,0:T(8,128)} %get-tuple-element.265) | copy-start | bytes 1775620
  469.9 10.6 %copy-start.30 = (f32[136,1088]{1,0:T(8,128)S(1)}, f32[136,1088]{1,0:T(8,128)}, u32[]{:S(2)}) copy-start(f32[136,1088]{1,0:T(8,128)} %param.28) | copy-start | bytes 1775620
  472.0 12.6 %collective-permute-start.1 = (f32[136,544]{1,0:T(8,128)}, f32[136,544]{1,0:T(8,128)}, u32[]{:S(2)}, u32[]{:S(2)}) collective-permute-start(f32[136,544]{1,0:T(8,128)} %get-tuple-element.219), channel_id=1, source_target_pairs={{0,1},{1,0},{2,3},{3,2},{4,5},{5,4},{6,7},{7,6},{8,9},{9,8},{10,11... | collective-permute-start | bytes 887816 | tf_op jit(solution)/shard_map/ppermute | solution.py:1045
  480.5 2.8 copy-start.20
  480.5 2.8 copy-start.33
  480.5 2.8 copy-start.34
  483.3 1.4 copy-start.9
  483.3 2.0 copy-start.28
  483.3 2.2 copy-start.29
  (5 other events, 4.9 us)
